TPU v7x, 256 devices: a whole 4x4x8 slice. The times are simulated.
256 devices in a mesh: grp: 8 (over y, core), col: 32 (over z, x).
Axes of the slice: x: 4, y: 4, z: 8, core: 2. Of those that a mesh axis runs over, the one named last changes fastest.
Arguments:
- amplitudes: bfloat16 [8, 2048, 1536], P('grp', 'col'), may hold values from -6 to 6
- ladder_int: bfloat16 [8, 1536, 1536], P('grp'), may hold values from -0.15625 to 0.15625
- pair_energy: float32 [8, 1536], P('grp'), may hold values from 0.75 to 1.5
- hole_energy: float32 [8, 2048], P('grp', 'col'), may hold values from 0.75 to 1.5
- pack_map: int32 [6144], P('col'), may hold values from 0 to 191, as said below
- unpack_map: int32 [6144], P('col'), may hold values from 0 to 191, as said below
- coupling_index: int32 [24, 16, 16], P('grp'), may hold values from 0 to 63
- coupling_table: float32 [64], replicated, may hold values from -0.2 to 0.2
- cycle_int: bfloat16 [24, 1024, 1024], P('grp'), may hold values from -0.005859375 to 0.005859375
- tile_list: int32 [8, 8], replicated, may hold values from 0 to 191, as said below
- tile_count: int32 [8], replicated, may hold values from 3 to 8, as said below
- slabs: bfloat16 [8, 8, 128, 1024], P('grp'), may hold values from -0.5 to 0.5
Outputs:
- doubles: bfloat16 [8, 2048, 1536], P('grp', 'col')
- triples: bfloat16 [8, 1024, 1024], P('grp', 'col')
Inputs may be any that keep to these rules, and one draw needn't show every extreme that they name: `pack_map`: each column block's 192 entries are a permutation of 0 to 191. `unpack_map`: each column block's 192 entries are a permutation of 0 to 191. `tile_list`: A panel id t lies in channel group t // 24. In each owner's list no channel group is named by more than 2 slots, and in every draw some owner names one group 2 times among its live slots. Slots at or past tile_count are ignored. `tile_count`: in every draw some owner has all 8 slots live and another has 3.
All inputs are finite; a program needn't handle non-finite values.
Results may differ from a plain program's by a relative error of at most 0.04.
Values may be sent and summed in bfloat16 or wider, within the bound.
A program may use at most 128 MiB of HBM per device.

v0:
```python
import jax
import jax.numpy as jnp
from jax import lax
from jax.sharding import PartitionSpec as P

MULT = 16
SEG = 512
TILE = 128
ITERS = 4


def body(
    amplitudes,
    ladder_int,
    pair_energy,
    hole_energy,
    pack_map,
    unpack_map,
    coupling_index,
    coupling_table,
    cycle_int,
    tile_list,
    tile_count,
    slabs,
):
    channels = cycle_int.shape[0]
    width_r = cycle_int.shape[1]
    col_count = lax.axis_size("col")
    ph_cols = width_r // col_count
    units = pack_map.shape[0]
    per_peer = units // col_count
    col_rows = amplitudes.shape[1]
    width_p = amplitudes.shape[2]
    table_size = coupling_table.shape[0]
    onehot = (coupling_index[..., None] == jnp.arange(table_size, dtype=jnp.int32)).astype(
        jnp.float32
    )
    coeffs = jnp.einsum("emnk,k->emn", onehot, coupling_table, precision=lax.Precision.HIGHEST)
    block_width = 128
    inner_blocks = block_width // MULT
    kron_blocks = jnp.einsum(
        "ab,emn->eanbm", jnp.eye(inner_blocks, dtype=jnp.float32), coeffs
    ).reshape(channels, block_width, block_width)
    kron_high = kron_blocks.astype(jnp.bfloat16)
    kron_low = (kron_blocks - kron_high.astype(jnp.float32)).astype(jnp.bfloat16)
    denom = pair_energy[0][None, :] + hole_energy[0][:, None]
    source = amplitudes[0].astype(jnp.float32)
    doubles = amplitudes
    cycle = jnp.zeros((ph_cols, channels, width_r), jnp.bfloat16)
    for iteration in range(ITERS):
        ladder = jnp.dot(doubles[0], ladder_int[0], preferred_element_type=jnp.float32)
        segments = doubles.reshape(units, SEG)
        outgoing = segments[pack_map]
        arrived = lax.all_to_all(
            outgoing.reshape(col_count, per_peer, SEG),
            "col",
            split_axis=0,
            concat_axis=0,
            tiled=True,
        )
        regrouped = arrived.reshape(units, SEG)[unpack_map].reshape(ph_cols, channels, width_r)
        count_rows = regrouped.shape[0]
        blocked = regrouped.reshape(count_rows, channels, width_r // block_width, block_width)
        mixed = jnp.einsum("ucbi,cij->ucbj", blocked, kron_high, preferred_element_type=jnp.float32)
        mixed = mixed + jnp.einsum(
            "ucbi,cij->ucbj", blocked, kron_low, preferred_element_type=jnp.float32
        )
        recoupled = (
            (blocked.astype(jnp.float32) + mixed)
            .reshape(count_rows, channels, width_r)
            .astype(jnp.bfloat16)
        )
        cycle_half = jnp.einsum(
            "ucr,crs->ucs", recoupled, cycle_int, preferred_element_type=jnp.float32
        ).astype(jnp.bfloat16)
        cycle = jnp.einsum(
            "ucx,xcr->ucr",
            cycle_half,
            lax.all_gather(recoupled, "col", axis=0, tiled=True),
            preferred_element_type=jnp.float32,
        ).astype(jnp.bfloat16)
        cycle_segments = cycle.reshape(units, SEG)
        slotted = jnp.zeros_like(cycle_segments).at[unpack_map].set(cycle_segments)
        coming_back = lax.all_to_all(
            slotted.reshape(col_count, per_peer, SEG),
            "col",
            split_axis=0,
            concat_axis=0,
            tiled=True,
        ).reshape(units, SEG)
        returned = (
            jnp.zeros_like(coming_back).at[pack_map].set(coming_back).reshape(col_rows, width_p)
        )
        doubles = ((source + ladder + returned.astype(jnp.float32)) / denom).astype(jnp.bfloat16)[
            None
        ]
    blocks_per = width_r // TILE
    slot_count = tile_list.shape[1]
    group_index = lax.axis_index("grp")
    my_list = lax.dynamic_index_in_dim(tile_list, group_index, 0, keepdims=False)
    my_count = lax.dynamic_index_in_dim(tile_count, group_index, 0, keepdims=False)
    slot_ids = jnp.arange(slot_count, dtype=jnp.int32)
    active = slot_ids < my_count
    my_slabs = slabs[0]
    piece = lax.all_gather(cycle, "grp", axis=1, tiled=True)
    start = jnp.int32(0)
    piece_channels = piece.shape[1]
    channel_ids = my_list // blocks_per
    block_ids = my_list % blocks_per
    inside = active & (channel_ids >= start) & (channel_ids < start + piece_channels)
    local_ids = jnp.clip(channel_ids, 0, piece_channels - 1) * blocks_per + block_ids
    flat_panels = piece.reshape(ph_cols, piece_channels * blocks_per, TILE)
    chosen = jnp.take(flat_panels, local_ids, axis=1) * inside.astype(jnp.bfloat16)[None, :, None]
    summed = jnp.einsum("usi,sin->un", chosen, my_slabs, preferred_element_type=jnp.float32)
    triples = summed.astype(jnp.bfloat16)[None]
    return (doubles, triples)


def solution(mesh):
    return jax.shard_map(
        body,
        mesh=mesh,
        in_specs=(
            P("grp", "col", None),
            P("grp", None, None),
            P("grp", None),
            P("grp", "col"),
            P("col"),
            P("col"),
            P("grp", None, None),
            P(),
            P("grp", None, None),
            P(),
            P(),
            P("grp", None, None, None),
        ),
        out_specs=(P("grp", "col", None), P("grp", "col", None)),
        check_vma=False,
    )
```

profile of v0, /device:TPU:1, one launch (start us, length us, event | category | flops | bytes accessed | tf_op | source)
XLA Modules:
  0.0 583.0 jit_solution(17860191367571201887)
XLA Ops:
  7.2 0.8 compare_select_fusion.1
  8.0 1.0 reshape.251
  9.0 1.0 gather_fusion
  10.0 0.8 reshape.252
  10.8 11.9 %all-to-all-start = ((bf16[32,6,512]{2,1,0:T(8,128)(2,1)}), bf16[32,6,512]{2,1,0:T(8,128)(2,1)S(1)}, u32[]{:S(2)}, u32[]{:S(2)}) async-start(bf16[32,6,512]{2,1,0:T(8,128)(2,1)} %reshape.252), calls=%async_computation | async-start | bytes 524288 | tf_op jit(solution)/shard_map/all_to_all | solution.py:54
  22.7 2.3 fusion.94
  25.1 1.4 multiply_bitcast_fusion
  26.5 0.7 compare_select_fusion
  27.2 1.8 reshape.254
  29.0 4.9 all-to-all-done
  34.1 1.0 gather_fusion.1
  35.6 0.7 copy.97
  36.4 84.8 %all-gather.6.cloned.1.call-done = bf16[1024,3,1024]{2,0,1:T(8,128)(2,1)} async-done(((bf16[32,3,1024]{2,0,1:T(8,128)(2,1)}), bf16[1024,3,1024]{2,0,1:T(8,128)(2,1)}) %all-gather.6.cloned.1.call-update) | async-done | bytes 6291472 | tf_op jit(solution)/shard_map/all_gather | solution.py:79
  121.2 6.9 %fusion.81 = bf16[32,3,1024]{2,0,1:T(8,128)(2,1)S(1)} fusion(bf16[1024,3,1024]{2,0,1:T(8,128)(2,1)} %all-gather.6.cloned.1.call-done, bf16[3,1024,1024]{2,1,0:T(8,128)(2,1)} %param.20, bf16[3,8,4,8,128]{4,3,2,1,0:T(8,128)(2,1)S(1)} %fusion.73), kind=kOutput, calls=%fused_computation.77 | convolution fusion | flops 402849792 | bytes 12976128 | tf_op jit(solution)/shard_map/ucx,xcr->ucr/dot_general | solution.py:76
  128.4 1.3 scatter_custom_fusion
  129.8 0.8 reshape.256
  130.5 5.6 all-to-all-start.1
  136.2 10.5 %all-to-all-done.1 = bf16[32,6,512]{2,1,0:T(8,128)(2,1)S(1)} async-done(((bf16[32,6,512]{2,1,0:T(8,128)(2,1)}), bf16[32,6,512]{2,1,0:T(8,128)(2,1)S(1)}, u32[]{:S(2)}, u32[]{:S(2)}) %all-to-all-start.1) | async-done | bytes 196640 | tf_op jit(solution)/shard_map/all_to_all | solution.py:84
  146.8 1.3 scatter_custom_fusion.1
  148.2 3.3 fusion.53
  151.6 1.0 gather_fusion.2
  152.7 15.5 %all_to_all.40 = bf16[32,6,512]{2,1,0:T(8,128)(2,1)S(1)} all-to-all(bf16[32,6,512]{2,1,0:T(8,128)(2,1)S(1)} %reshape.258), channel_id=1, replica_groups=mesh['grp'=8,'col'=32] {'col'}, dimensions={0} | all-to-all | bytes 393216 | tf_op jit(solution)/shard_map/all_to_all | solution.py:54
  168.2 1.0 gather_fusion.3
  169.8 0.7 copy.96
  170.8 85.3 %all-gather.8.cloned.1.call-done = bf16[1024,3,1024]{2,0,1:T(8,128)(2,1)} async-done(((bf16[32,3,1024]{2,0,1:T(8,128)(2,1)}), bf16[1024,3,1024]{2,0,1:T(8,128)(2,1)}) %all-gather.8.cloned.1.call-update) | async-done | bytes 6291472 | tf_op jit(solution)/shard_map/all_gather | solution.py:79
  256.1 6.9 %fusion.82 = bf16[32,3,1024]{2,0,1:T(8,128)(2,1)S(1)} fusion(bf16[1024,3,1024]{2,0,1:T(8,128)(2,1)} %all-gather.8.cloned.1.call-done, bf16[3,1024,1024]{2,1,0:T(8,128)(2,1)} %param.20, bf16[3,8,4,8,128]{4,3,2,1,0:T(8,128)(2,1)S(1)} %fusion.74), kind=kOutput, calls=%fused_computation.78 | convolution fusion | flops 402849792 | bytes 12976128 | tf_op jit(solution)/shard_map/ucx,xcr->ucr/dot_general | solution.py:76
  263.3 1.3 scatter_custom_fusion.2
  264.8 16.0 %all_to_all.41 = bf16[32,6,512]{2,1,0:T(8,128)(2,1)S(1)} all-to-all(bf16[32,6,512]{2,1,0:T(8,128)(2,1)S(1)} %reshape.261), channel_id=1, replica_groups=mesh['grp'=8,'col'=32] {'col'}, dimensions={0} | all-to-all | bytes 393216 | tf_op jit(solution)/shard_map/all_to_all | solution.py:84
  280.8 1.3 scatter_custom_fusion.3
  282.1 0.8 reshape.275
  283.0 3.4 fusion.50
  286.4 1.0 gather_fusion.4
  287.5 15.6 %all_to_all.42 = bf16[32,6,512]{2,1,0:T(8,128)(2,1)} all-to-all(bf16[32,6,512]{2,1,0:T(8,128)(2,1)S(1)} %reshape.263), channel_id=1, replica_groups=mesh['grp'=8,'col'=32] {'col'}, dimensions={0} | all-to-all | bytes 393216 | tf_op jit(solution)/shard_map/all_to_all | solution.py:54
  303.1 1.0 reshape.264
  304.1 1.0 gather_fusion.5
  305.6 0.7 copy.95
  306.4 85.5 %all-gather.10.cloned.1.call-done = bf16[1024,3,1024]{2,0,1:T(8,128)(2,1)} async-done(((bf16[32,3,1024]{2,0,1:T(8,128)(2,1)}), bf16[1024,3,1024]{2,0,1:T(8,128)(2,1)}) %all-gather.10.cloned.1.call-update) | async-done | bytes 6291472 | tf_op jit(solution)/shard_map/all_gather | solution.py:79
  391.9 6.9 %fusion.83 = bf16[32,3,1024]{2,0,1:T(8,128)(2,1)S(1)} fusion(bf16[1024,3,1024]{2,0,1:T(8,128)(2,1)} %all-gather.10.cloned.1.call-done, bf16[3,1024,1024]{2,1,0:T(8,128)(2,1)} %param.20, bf16[3,8,4,8,128]{4,3,2,1,0:T(8,128)(2,1)S(1)} %fusion.75), kind=kOutput, calls=%fused_computation.79 | convolution fusion | flops 402849792 | bytes 12976128 | tf_op jit(solution)/shard_map/ucx,xcr->ucr/dot_general | solution.py:76
  399.2 1.3 scatter_custom_fusion.4
  400.6 16.1 %all_to_all.43 = bf16[32,6,512]{2,1,0:T(8,128)(2,1)} all-to-all(bf16[32,6,512]{2,1,0:T(8,128)(2,1)S(1)} %reshape.266), channel_id=1, replica_groups=mesh['grp'=8,'col'=32] {'col'}, dimensions={0} | all-to-all | bytes 393216 | tf_op jit(solution)/shard_map/all_to_all | solution.py:84
  416.7 1.0 reshape.394
  417.7 1.5 scatter_custom_fusion.5
  419.3 0.8 reshape.276
  420.1 3.4 fusion.47
  423.6 1.0 gather_fusion.6
  424.6 15.5 %all_to_all.44 = bf16[32,6,512]{2,1,0:T(8,128)(2,1)S(1)} all-to-all(bf16[32,6,512]{2,1,0:T(8,128)(2,1)S(1)} %reshape.268), channel_id=1, replica_groups=mesh['grp'=8,'col'=32] {'col'}, dimensions={0} | all-to-all | bytes 393216 | tf_op jit(solution)/shard_map/all_to_all | solution.py:54
  440.2 1.0 gather_fusion.7
  441.7 0.7 copy.94
  442.5 85.5 %all-gather.12.cloned.1.call-done = bf16[1024,3,1024]{2,0,1:T(8,128)(2,1)} async-done(((bf16[32,3,1024]{2,0,1:T(8,128)(2,1)}), bf16[1024,3,1024]{2,0,1:T(8,128)(2,1)}) %all-gather.12.cloned.1.call-update) | async-done | bytes 6291472 | tf_op jit(solution)/shard_map/all_gather | solution.py:79
  528.0 7.6 %fusion.84 = bf16[32,3,1024]{2,0,1:T(8,128)(2,1)} fusion(bf16[1024,3,1024]{2,0,1:T(8,128)(2,1)} %all-gather.12.cloned.1.call-done, bf16[3,1024,1024]{2,1,0:T(8,128)(2,1)} %param.20, bf16[3,8,4,8,128]{4,3,2,1,0:T(8,128)(2,1)S(1)} %fusion.76), kind=kOutput, calls=%fused_computation.80 | convolution fusion | flops 402849792 | bytes 12976128 | tf_op jit(solution)/shard_map/ucx,xcr->ucr/dot_general | solution.py:76
  536.2 1.3 and_convert_fusion
  537.6 1.1 copy.55
  538.9 1.3 scatter_custom_fusion.6
  540.2 0.8 reshape.271
  540.9 5.6 all-to-all-start.7
  546.6 0.7 fusion.139
  547.3 9.8 %all-to-all-done.7 = bf16[32,6,512]{2,1,0:T(8,128)(2,1)S(1)} async-done(((bf16[32,6,512]{2,1,0:T(8,128)(2,1)}), bf16[32,6,512]{2,1,0:T(8,128)(2,1)S(1)}, u32[]{:S(2)}, u32[]{:S(2)}) %all-to-all-start.7) | async-done | bytes 196640 | tf_op jit(solution)/shard_map/all_to_all | solution.py:84
  557.2 1.3 scatter_custom_fusion.7
  558.6 4.0 fusion.56
  562.6 3.4 copy.56
  566.0 3.7 reshape.273
  569.7 3.6 copy.57
  573.3 2.0 gather_fusion.8
  575.3 1.1 fusion.91
  (65 shorter events, 5.9 us)
Async XLA Ops:
  7.2 568.1 %copy-start = (bf16[1,8,128,1024]{3,2,1,0:T(8,128)(2,1)S(1)}, bf16[1,8,128,1024]{3,2,1,0:T(8,128)(2,1)}, u32[]{:S(2)}) copy-start(bf16[1,8,128,1024]{3,2,1,0:T(8,128)(2,1)} %param.23) | copy-start | bytes 6291460
  10.8 23.2 %all-to-all-start = ((bf16[32,6,512]{2,1,0:T(8,128)(2,1)}), bf16[32,6,512]{2,1,0:T(8,128)(2,1)S(1)}, u32[]{:S(2)}, u32[]{:S(2)}) async-start(bf16[32,6,512]{2,1,0:T(8,128)(2,1)} %reshape.252), calls=%async_computation | async-start | bytes 524288 | tf_op jit(solution)/shard_map/all_to_all | solution.py:54
  22.7 98.5 %all-gather.6.cloned.1.call-start = ((), (), s32[]{:S(2)}) async-start(), calls=%async_computation.8 | async-start | bytes 6488064 | tf_op jit(solution)/shard_map/all_gather | solution.py:79
  36.3 99.8 %copy-start.3 = (f32[1,1536]{1,0:T(1,128)S(1)}, f32[1,1536]{1,0:T(1,128)}, u32[]{:S(2)}) copy-start(f32[1,1536]{1,0:T(1,128)} %param.14) | copy-start | bytes 18436
  36.4 111.9 %copy-start.1 = (bf16[1,64,1536]{2,1,0:T(8,128)(2,1)S(1)}, bf16[1,64,1536]{2,1,0:T(8,128)(2,1)}, u32[]{:S(2)}) copy-start(bf16[1,64,1536]{2,1,0:T(8,128)(2,1)} %param.12) | copy-start | bytes 589828
  36.4 111.8 %copy-start.2 = (f32[1,64]{1,0:T(1,128)S(1)}, f32[1,64]{1,0:T(1,128)}, u32[]{:S(2)}) copy-start(f32[1,64]{1,0:T(1,128)} %param.15) | copy-start | bytes 772
  130.5 16.2 %all-to-all-start.1 = ((bf16[32,6,512]{2,1,0:T(8,128)(2,1)}), bf16[32,6,512]{2,1,0:T(8,128)(2,1)S(1)}, u32[]{:S(2)}, u32[]{:S(2)}) async-start(bf16[32,6,512]{2,1,0:T(8,128)(2,1)} %reshape.256), calls=%async_computation.1 | async-start | bytes 524288 | tf_op jit(solution)/shard_map/all_to_all | solution.py:84
  136.1 119.9 %all-gather.8.cloned.1.call-start = ((), (), s32[]{:S(2)}) async-start(), calls=%async_computation.9 | async-start | bytes 6488064 | tf_op jit(solution)/shard_map/all_gather | solution.py:79
  170.5 221.4 %all-gather.10.cloned.1.call-start = ((), (), s32[]{:S(2)}) async-start(), calls=%async_computation.10 | async-start | bytes 6488064 | tf_op jit(solution)/shard_map/all_gather | solution.py:79
  306.4 221.6 %all-gather.12.cloned.1.call-start = ((), (), s32[]{:S(2)}) async-start(), calls=%async_computation.11 | async-start | bytes 6488064 | tf_op jit(solution)/shard_map/all_gather | solution.py:79
  442.5 93.1 %copy-start.4 = (s32[8]{0:T(128)S(1)}, s32[8]{0:T(128)}, u32[]{:S(2)}) copy-start(s32[8]{0:T(128)} %param.22) | copy-start | bytes 100
  442.5 120.1 %all-gather.14.cloned.1.call-start = ((), (), s32[]{:S(2)}) async-start(), calls=%async_computation.12 | async-start | bytes 1769472 | tf_op jit(solution)/shard_map/all_gather | solution.py:105
  540.9 16.2 %all-to-all-start.7 = ((bf16[32,6,512]{2,1,0:T(8,128)(2,1)}), bf16[32,6,512]{2,1,0:T(8,128)(2,1)S(1)}, u32[]{:S(2)}, u32[]{:S(2)}) async-start(bf16[32,6,512]{2,1,0:T(8,128)(2,1)} %reshape.271), calls=%async_computation.7 | async-start | bytes 524288 | tf_op jit(solution)/shard_map/all_to_all | solution.py:84
Sparse Core Ops, SparseCore 0:
  36.5 84.6 all-gather.5
  170.7 85.3 all-gather.7
  306.5 85.3 all-gather.9
  442.6 85.3 all-gather.11
  535.7 25.0 all-gather.13
where the time goes:
time: 586 us; the launch traced here: 583 us
  waiting for transfers between devices  366 us (62%)
  blocking collectives  78.5 us (13%)
  local copies, waits for them, and re-layouts  48 us (8%)
  matrix products  47.1 us (8%)
  starting transfers between devices  23.5 us (4%)
  between operations  14.3 us (2%)
    all_gather x4, waiting for transfers between devices, body(): lax.all_gather(recoupled, 'col', axis=0, tiled=True)  341 us
    all_to_all x3, blocking collectives, body(): lax.all_to_all(outgoing.reshape(col_count, per_peer, SEG), 'col', split_a...  46.5 us
    all_to_all x2, blocking collectives, body(): lax.all_to_all(slotted.reshape(col_count, per_peer, SEG), 'col', split_ax...  32.1 us
    dot_general x4, matrix products, body(): jnp.einsum('ucx,xcr->ucr', cycle_half, lax.all_gather(recoupled, 'col', a...  28.2 us
    all_to_all x2, waiting for transfers between devices, body(): lax.all_to_all(slotted.reshape(col_count, per_peer, SEG), 'col', split_ax...  20.3 us
    dot_general x4, matrix products, body(): jnp.dot(doubles[0], ladder_int[0], preferred_element_type=jnp.float32)  13.9 us
    all_to_all x1, starting transfers between devices, body(): lax.all_to_all(outgoing.reshape(col_count, per_peer, SEG), 'col', split_a...  11.9 us
  transfers between devices with their start and end apart: 8, of which 7 were waited for; matrix products, arithmetic and copies ran while one was open for 3% of the time, Pallas kernels for 0%

commit v1 on v0

v1 whole, which is shorter than its diff:
```python
import functools

import jax
import jax.numpy as jnp
from jax import lax
from jax.experimental import pallas as pl
from jax.experimental.pallas import tpu as pltpu
from jax.sharding import PartitionSpec as P

MULT = 16
SEG = 512
TILE = 128
ITERS = 4
NX = 4
NZ = 8
PER = 6
ZROWS = NX * PER
UNITS = 192
PLANE = NX * UNITS
ROWS = 32
CHUNK = NX * ROWS
PH = 3
MESH = pl.DeviceIdType.MESH
F32 = jnp.float32
BF16 = jnp.bfloat16


def dot(a, b):
    return jnp.dot(a, b, preferred_element_type=F32)


def kernel(
    n_grp,
    amp,
    pair_e,
    hole_e,
    pack_row,
    pack_col,
    slots_own,
    coef_index,
    table,
    tile_list,
    tile_count,
    w_hbm,
    l_hbm,
    slab_hbm,
    d_out,
    t_out,
    w,
    lint,
    slab,
    kron,
    slots,
    perm,
    perm_t,
    pack,
    pack_t,
    doubles,
    ladder,
    packed,
    segs,
    cols,
    panel,
    xrow,
    half,
    cyc,
    slotted,
    back_z,
    back_x,
    own_rows,
    pick,
    picked,
    local_sem,
    slots_sem,
    fz_sem,
    fk_sem,
    fx_sem,
    ring_sem,
    bz_sem,
    bx_sem,
    tx_sem,
    tg_sem,
):
    me = lax.axis_index("col")
    g = lax.axis_index("grp")
    z = me // NX
    x = me % NX

    def at_z(d):
        return (z + d + NZ) % NZ

    def at_x(d):
        return (x + d + NX) % NX

    def remote(src, dst, sems, index, grp, zz, xx):
        return pltpu.make_async_remote_copy(
            src_ref=src,
            dst_ref=dst,
            send_sem=sems.at[(0,) + index],
            recv_sem=sems.at[(1,) + index],
            device_id=(grp, zz * NX + xx),
            device_id_type=MESH,
        )

    loads = [
        pltpu.make_async_copy(l_hbm, lint, local_sem.at[0]),
        pltpu.make_async_copy(w_hbm, w, local_sem.at[1]),
        pltpu.make_async_copy(slab_hbm, slab, local_sem.at[2]),
    ]
    for load in loads:
        load.start()

    barrier = pltpu.get_barrier_semaphore()
    for d in range(1, NZ):
        pl.semaphore_signal(
            barrier, inc=1, device_id=(g, at_z(d) * NX + x), device_id_type=MESH
        )
    for d in range(1, NX):
        pl.semaphore_signal(
            barrier, inc=1, device_id=(g, z * NX + at_x(d)), device_id_type=MESH
        )
    for d in range(1, n_grp):
        pl.semaphore_signal(
            barrier, inc=1, device_id=((g + d) % n_grp, me), device_id_type=MESH
        )

    lane_k = lax.broadcasted_iota(jnp.int32, (UNITS, UNITS), 1)
    row_k = lax.broadcasted_iota(jnp.int32, (UNITS, UNITS), 0)
    lane_k = (lane_k % 64) * 3 + lane_k // 64
    row_k = (row_k % 64) * 3 + row_k // 64
    pack[...] = (pack_col[...] == lane_k).astype(F32).astype(BF16)
    pack_t[...] = (pack_row[...] == row_k).astype(F32).astype(BF16)
    for t in range(3):
        doubles[t * 64 : (t + 1) * 64, :] = amp[:, t * SEG : (t + 1) * SEG]

    pl.semaphore_wait(barrier, (NZ - 1) + (NX - 1) + (n_grp - 1))

    def slots_copy(d, to):
        return remote(
            slots_own, slots.at[x if to else at_x(-d)], slots_sem, (d,), g, z, at_x(d)
        )

    for d in range(1, NX):
        slots_copy(d, True).start()
    slots[x] = slots_own[...]

    def forward_z(d, to):
        target = at_z(d)
        return remote(
            packed.at[target], segs.at[z if to else at_z(-d), x], fz_sem, (d,), g, target, x
        )

    def send_packed():
        value = dot(pack[...], doubles[...])
        for zz in range(NZ):
            packed[zz] = value[zz * ZROWS : (zz + 1) * ZROWS, :].astype(BF16)
        for d in (4, 3, 5, 2, 6, 1, 7):
            forward_z(d, True).start()
        segs[z, x] = packed[z]

    def ladder_part():
        for t in range(3):
            acc = None
            for k in range(3):
                part = dot(
                    doubles[k * 64 : (k + 1) * 64, :],
                    lint[k * SEG : (k + 1) * SEG, t * SEG : (t + 1) * SEG],
                )
                acc = part if acc is None else acc + part
            ladder[:, t * SEG : (t + 1) * SEG] = acc

    def forward_k(d, to):
        target = at_x(d)
        lanes = pl.ds(pl.multiple_of(target * TILE, TILE), TILE)
        return remote(
            segs.at[:, x, :, lanes],
            cols.at[:, x if to else at_x(-d)],
            fk_sem,
            (d,),
            g,
            z,
            target,
        )

    def forward_x(d, to):
        source = x if to else at_x(-d)
        return remote(
            segs.at[:, x], segs.at[:, source], fx_sem, (d,), g, z, at_x(d)
        )

    def ring(way, step, e, to):
        sign = 1 if way == 0 else -1
        chunk = at_z(-sign * (step - 1)) if to else at_z(-sign * step)
        if step < 4:
            rows = pl.ds(pl.multiple_of(chunk * CHUNK, CHUNK), CHUNK)
        else:
            rows = pl.ds(pl.multiple_of(chunk * CHUNK + way * 64, 64), 64)
        ref = panel.at[e, rows, :]
        return remote(ref, ref, ring_sem, (way, step - 1, e), g, at_z(sign), x)

    def recouple(value, e):
        mixed = dot(value.astype(BF16), kron[e])
        return (value + (mixed[:, :TILE] + mixed[:, TILE:])).astype(BF16)

    def row_part(e):
        found = dot(
            perm[e * 256 : (e + 1) * 256, :],
            segs[...].reshape(PLANE, SEG),
        )
        stacked = jnp.concatenate(
            [found[:, q * TILE : (q + 1) * TILE] for q in range(4)], axis=0
        )
        done = recouple(stacked, e)
        for q in range(4):
            for h in range(2):
                xrow[e, :, (h * 4 + q) * TILE : (h * 4 + q + 1) * TILE] = done[
                    q * 256 + h * CHUNK : q * 256 + (h + 1) * CHUNK, :
                ]

    def half_part(e):
        half[e] = dot(xrow[e], w[e]).astype(BF16)

    def backward_z(d, to):
        target = at_z(d)
        return remote(
            slotted.at[target],
            back_z.at[z if to else at_z(-d)],
            bz_sem,
            (d,),
            g,
            target,
            x,
        )

    def backward_x(d, to):
        target = at_x(d)
        return remote(
            back_z.at[:, target],
            back_x.at[x if to else at_x(-d)],
            bx_sem,
            (d,),
            g,
            z,
            target,
        )

    def own_copy(d, to):
        target = at_x(d)
        return remote(
            cyc.at[:, target],
            own_rows.at[x if to else at_x(-d)],
            tx_sem,
            (d,),
            g,
            z,
            target,
        )

    def group_copy(d, to):
        target = (g + d) % n_grp
        source = g if to else (g - d + n_grp) % n_grp
        return remote(pick.at[d], picked.at[source], tg_sem, (d,), target, z, x)

    send_packed()

    def coef_step(k, acc):
        return jnp.where(coef_index[...] == k, table[k], acc)

    coefs = lax.fori_loop(
        0, table.shape[0], coef_step, jnp.zeros((PH, TILE, TILE), F32)
    )
    same = (
        lax.broadcasted_iota(jnp.int32, (PH, TILE, TILE), 1) // MULT
        == lax.broadcasted_iota(jnp.int32, (PH, TILE, TILE), 2) // MULT
    )
    coefs = jnp.where(same, coefs, 0.0)
    high = coefs.astype(BF16)
    kron[:, :, :TILE] = high
    kron[:, :, TILE:] = (coefs - high.astype(F32)).astype(BF16)

    for d in range(1, NX):
        slots_copy(d, False).wait_recv()
    lane_x = lax.broadcasted_iota(jnp.int32, (8, TILE), 1) // ROWS
    place = jnp.zeros((8, TILE), F32)
    for xx in range(NX):
        place = jnp.where(lane_x == xx, slots[xx] + float(PER * xx), place)
    for k in range(2 * PH):
        line = place[k : k + 1, :]
        index = lax.broadcasted_iota(jnp.int32, (PLANE, TILE), 0).astype(F32)
        perm_t[:, k * TILE : (k + 1) * TILE] = (index == line).astype(F32).astype(BF16)
        column = jnp.transpose(jnp.broadcast_to(line, (TILE, TILE)))
        for b in range(PLANE // TILE):
            lanes = lax.broadcasted_iota(jnp.int32, (TILE, TILE), 1) + b * TILE
            perm[k * TILE : (k + 1) * TILE, b * TILE : (b + 1) * TILE] = (
                (column == lanes.astype(F32)).astype(F32).astype(BF16)
            )

    loads[0].wait()

    def iteration(it, carry):
        @pl.when(it > 0)
        def _():
            send_packed()

        ladder_part()
        for d in (1, 7, 2, 6, 3, 5, 4):
            forward_z(d, False).wait_recv()
        for d in (2, 1, 3):
            forward_k(d, True).start()
        for d in (2, 1, 3):
            forward_x(d, True).start()
        cols[:, x] = segs[:, x, :, pl.ds(pl.multiple_of(x * TILE, TILE), TILE)]
        for d in (1, 3, 2):
            forward_k(d, False).wait_recv()
        found = dot(perm[...], cols[...].reshape(PLANE, TILE))
        for e in range(PH):
            done = recouple(found[e * 256 : (e + 1) * 256, :], e)
            rows = pl.ds(pl.multiple_of(z * CHUNK, CHUNK), CHUNK)
            panel[e, rows, :TILE] = done[:CHUNK, :]
            panel[e, rows, TILE:] = done[CHUNK:, :]
            ring(0, 1, e, True).start()
            ring(1, 1, e, True).start()
        for e in range(PH):
            for way in range(2):
                ring(way, 1, e, False).wait_recv()
                ring(way, 2, e, True).start()
        for d in (1, 3, 2):
            forward_x(d, False).wait_recv()

        @pl.when(it == 0)
        def _():
            loads[1].wait()

        for e in range(PH):
            for way in range(2):
                ring(way, 2, e, False).wait_recv()
                ring(way, 3, e, True).start()
            row_part(e)
        for e in range(PH):
            for way in range(2):
                ring(way, 3, e, False).wait_recv()
                ring(way, 4, e, True).start()
            half_part(e)
        for e in range(PH):
            for way in range(2):
                ring(way, 4, e, False).wait_recv()
            block = dot(half[e], panel[e])
            for h in range(2):
                cyc[2 * e + h] = (
                    block[:, h * TILE : (h + 1) * TILE]
                    .reshape(NX, ROWS, TILE)
                    .astype(BF16)
                )
        value = dot(perm_t[...], cyc[...].reshape(PLANE, TILE))
        slotted[...] = value.reshape(NZ, NX, ZROWS, TILE).astype(BF16)
        for d in range(1, NX):
            forward_k(d, True).wait_send()
            forward_x(d, True).wait_send()
        for d in (4, 3, 5, 2, 6, 1, 7):
            backward_z(d, True).start()
        back_z[z] = slotted[z]

        @pl.when(it == ITERS - 1)
        def _():
            for d in (2, 1, 3):
                own_copy(d, True).start()
            own_rows[x] = cyc[:, x]

        for d in (1, 7, 2, 6, 3, 5, 4):
            backward_z(d, False).wait_recv()
        for d in (2, 1, 3):
            backward_x(d, True).start()
        back_x[x] = back_z[:, x]

        @pl.when(it == ITERS - 1)
        def _():
            for d in (1, 3, 2):
                own_copy(d, False).wait_recv()
            for d in range(n_grp):
                owner = (g + d) % n_grp
                count = jnp.int32(0)
                first = jnp.int32(0)
                second = jnp.int32(0)
                for s in range(tile_list.shape[1]):
                    tile = tile_list[owner, s]
                    mine = tile // 24 == g
                    local = tile - g * 24
                    blk = local % 8
                    where = (blk % 4) * (2 * PH) + (local // 8) * 2 + blk // 4
                    first = jnp.where(mine & (count == 0), where, first)
                    second = jnp.where(mine & (count == 1), where, second)
                    count = count + jnp.where(mine, 1, 0)
                flat = own_rows.reshape(NX * 2 * PH, ROWS, TILE)
                if d == 0:
                    picked[g, 0] = flat[first]
                    picked[g, 1] = flat[second]
                else:
                    pick[d, 0] = flat[first]
                    pick[d, 1] = flat[second]
                    group_copy(d, True).start()

        for d in (1, 3, 2):
            backward_x(d, False).wait_recv()
        together = jnp.concatenate(
            [back_x[xx].reshape(UNITS, TILE) for xx in range(NX)], axis=1
        )
        returned = dot(pack_t[...], together)
        for t in range(3):
            lanes = slice(t * SEG, (t + 1) * SEG)
            total = (amp[:, lanes].astype(F32) + ladder[:, lanes]) + returned[
                t * 64 : (t + 1) * 64, :
            ]
            doubles[t * 64 : (t + 1) * 64, :] = (
                total / (pair_e[:, lanes] + hole_e[...])
            ).astype(BF16)

        for d in range(1, NZ):
            forward_z(d, True).wait_send()
            backward_z(d, True).wait_send()
        for d in range(1, NX):
            backward_x(d, True).wait_send()
        for step in range(1, 5):
            for e in range(PH):
                for way in range(2):
                    ring(way, step, e, True).wait_send()
        return carry

    lax.fori_loop(0, ITERS, iteration, jnp.int32(0))

    for t in range(3):
        d_out[:, t * SEG : (t + 1) * SEG] = doubles[t * 64 : (t + 1) * 64, :]

    for d in range(1, n_grp):
        group_copy(d, False).wait_recv()
    loads[2].wait()
    live = tile_count[g]
    flat = picked.reshape(n_grp * 2, ROWS, TILE)
    parts = []
    for s in range(tile_list.shape[1]):
        group = tile_list[g, s] // 24
        rank = jnp.int32(0)
        for before in range(s):
            rank = rank + jnp.where(tile_list[g, before] // 24 == group, 1, 0)
        part = flat[group * 2 + jnp.minimum(rank, 1)]
        parts.append(
            (part.astype(F32) * jnp.where(s < live, 1.0, 0.0).astype(F32)).astype(BF16)
        )
    t_out[...] = dot(jnp.concatenate(parts, axis=1), slab[...]).astype(BF16)

    for d in range(1, NX):
        slots_copy(d, True).wait_send()
        own_copy(d, True).wait_send()
    for d in range(1, n_grp):
        group_copy(d, True).wait_send()


def body(
    amplitudes,
    ladder_int,
    pair_energy,
    hole_energy,
    pack_map,
    unpack_map,
    coupling_index,
    coupling_table,
    cycle_int,
    tile_list,
    tile_count,
    slabs,
):
    n_grp = lax.axis_size("grp")
    width_p = amplitudes.shape[2]
    width_r = cycle_int.shape[1]
    slot = (unpack_map // PER) * ZROWS + unpack_map % PER
    slot = slot.reshape(ROWS, 2 * PH).transpose(1, 0).astype(F32)
    slots_own = jnp.pad(jnp.tile(slot, (1, NX)), ((0, 2), (0, 0)))
    coef_index = jnp.tile(jnp.swapaxes(coupling_index, 1, 2), (1, 8, 8))

    vmem = pl.BlockSpec(memory_space=pltpu.VMEM)
    smem = pl.BlockSpec(memory_space=pltpu.SMEM)
    anywhere = pl.BlockSpec(memory_space=pl.ANY)
    dma = pltpu.SemaphoreType.DMA
    doubles, triples = pl.pallas_call(
        functools.partial(kernel, n_grp),
        out_shape=(
            jax.ShapeDtypeStruct((64, width_p), BF16),
            jax.ShapeDtypeStruct((ROWS, width_r), BF16),
        ),
        in_specs=[vmem] * 7 + [smem] * 3 + [anywhere] * 3,
        out_specs=(vmem, vmem),
        scratch_shapes=[
            pltpu.VMEM((PH, width_r, width_r), BF16),
            pltpu.VMEM((width_p, width_p), BF16),
            pltpu.VMEM((width_r, width_r), BF16),
            pltpu.VMEM((PH, TILE, 2 * TILE), BF16),
            pltpu.VMEM((NX, 8, TILE), F32),
            pltpu.VMEM((PLANE, PLANE), BF16),
            pltpu.VMEM((PLANE, PLANE), BF16),
            pltpu.VMEM((UNITS, UNITS), BF16),
            pltpu.VMEM((UNITS, UNITS), BF16),
            pltpu.VMEM((UNITS, SEG), BF16),
            pltpu.VMEM((64, width_p), F32),
            pltpu.VMEM((NZ, ZROWS, SEG), BF16),
            pltpu.VMEM((NZ, NX, ZROWS, SEG), BF16),
            pltpu.VMEM((NZ, NX, ZROWS, TILE), BF16),
            pltpu.VMEM((PH, width_r, 2 * TILE), BF16),
            pltpu.VMEM((PH, CHUNK, width_r), BF16),
            pltpu.VMEM((PH, CHUNK, width_r), BF16),
            pltpu.VMEM((2 * PH, NX, ROWS, TILE), BF16),
            pltpu.VMEM((NZ, NX, ZROWS, TILE), BF16),
            pltpu.VMEM((NZ, NX, ZROWS, TILE), BF16),
            pltpu.VMEM((NX, NZ, ZROWS, TILE), BF16),
            pltpu.VMEM((NX, 2 * PH, ROWS, TILE), BF16),
            pltpu.VMEM((n_grp, 2, ROWS, TILE), BF16),
            pltpu.VMEM((n_grp, 2, ROWS, TILE), BF16),
            dma((3,)),
            dma((2, NX)),
            dma((2, NZ)),
            dma((2, NX)),
            dma((2, NX)),
            dma((2, 2, 4, PH)),
            dma((2, NZ)),
            dma((2, NX)),
            dma((2, NX)),
            dma((2, n_grp)),
        ],
        compiler_params=pltpu.CompilerParams(
            collective_id=0, has_side_effects=True, vmem_limit_bytes=60 * 1024 * 1024
        ),
    )(
        amplitudes[0],
        pair_energy,
        hole_energy.reshape(-1, 1),
        pack_map.reshape(1, -1),
        pack_map.reshape(-1, 1),
        slots_own,
        coef_index,
        coupling_table,
        tile_list,
        tile_count,
        cycle_int,
        ladder_int[0],
        slabs.reshape(width_r, width_r),
    )
    return doubles[None], triples[None]


def solution(mesh):
    return jax.shard_map(
        body,
        mesh=mesh,
        in_specs=(
            P("grp", "col", None),
            P("grp", None, None),
            P("grp", None),
            P("grp", "col"),
            P("col"),
            P("col"),
            P("grp", None, None),
            P(),
            P("grp", None, None),
            P(),
            P(),
            P("grp", None, None, None),
        ),
        out_specs=(P("grp", "col", None), P("grp", "col", None)),
        check_vma=False,
    )
```

time: 586 us -> 195 us (0.33)
  waiting for transfers between devices: 366 us -> 0 us
  Pallas kernels: 0 us -> 184 us
  blocking collectives: 78.5 us -> 0 us
  matrix products: 47.1 us -> 0 us
  local copies, waits for them, and re-layouts: 48 us -> 8.83 us
  starting transfers between devices: 23.5 us -> 0 us
  between operations: 14.3 us -> 0.66 us
    all_gather x5 -> x0, waiting for transfers between devices: 341 us -> none  [the longest x4 341 us: body(): lax.all_gather(recoupled, 'col', axis=0, tiled=True)]
    pallas_call x0 -> x1, Pallas kernels: none -> 184 us  [body(): pl.pallas_call(functools.partial(kernel, n_grp), out_shape=(jax.ShapeDtyp...]
    all_to_all x5 -> x0, blocking collectives: 78.5 us -> none  [the longest x3 46.5 us: body(): lax.all_to_all(outgoing.reshape(col_count, per_peer, SEG), 'col', split_a...]
    dot_general x18 -> x0, matrix products: 47.1 us -> none  [the longest x4 28.2 us: body(): jnp.einsum('ucx,xcr->ucr', cycle_half, lax.all_gather(recoupled, 'col', a...]
    all_to_all x3 -> x0, waiting for transfers between devices: 25.3 us -> none  [the longest x2 20.3 us: body(): lax.all_to_all(slotted.reshape(col_count, per_peer, SEG), 'col', split_ax...]
    all_to_all x3 -> x0, starting transfers between devices: 23.1 us -> none  [the longest x1 11.9 us: body(): lax.all_to_all(outgoing.reshape(col_count, per_peer, SEG), 'col', split_a...]
    reshape x24 -> x2, local copies, waits for them, and re-layouts: 16 us -> 2.79 us  [the longest x1 1.43 us: body(): pack_map.reshape(-1, 1)]
    scatter x8 -> x0, local copies, waits for them, and re-layouts: 10.8 us -> none  [the longest x4 5.52 us: body(): jnp.zeros_like(coming_back).at[pack_map].set(coming_back)]
  transfers between devices with their start and end apart: 8 -> 0, of which waited for: 7 -> 0; matrix products, arithmetic and copies ran while one was open for 3% -> 0% of each run, Pallas kernels for 0% -> 0%
where the time goes in v1:
time: 195 us; the launch traced here: 194 us
  Pallas kernels  184 us (94%)
  local copies, waits for them, and re-layouts  8.83 us (5%)
    pallas_call x1, Pallas kernels, body(): pl.pallas_call(functools.partial(kernel, n_grp), out_shape=(jax.ShapeDtyp...  184 us

profile of v1, /device:TPU:1, one launch (start us, length us, event | category | flops | bytes accessed | tf_op | source)
XLA Modules:
  0.0 194.3 jit_solution(17713871258519688218)
XLA Ops:
  0.6 0.8 copy.17
  1.4 0.2 tile.20
  1.6 1.1 tile.21.coef_index
  2.7 1.4 copy.19.pack_col
  4.2 0.7 fusion.1
  4.8 0.1 convert_element_type.12
  4.9 0.1 copy.16
  5.0 0.1 tile.9
  5.1 0.6 pad.4.slots_own
  5.7 1.4 copy.18.hole_e
  7.1 184.1 %shard_map.131 = (bf16[64,1536]{1,0:T(8,128)(2,1)}, bf16[32,1024]{1,0:T(8,128)(2,1)}) custom-call(bf16[64,1536]{1,0:T(8,128)(2,1)} %bitcast.15, f32[1,1536]{1,0:T(1,128)} %pair_e.1, f32[64,1]{1,0:T(8,128)} %copy.18.hole_e, s32[1,192]{1,0:T(1,128)} %bitcast.20, s32[192,1]{1,0:T(8,128)} %copy.19.pack_col, f32[8,128]{1,0:T(8,128)} %pad.4.slots_own, ...), custom_call_target="tpu_custom_call" | custom-call | tf_op jit(solution)/shard_map/pallas_call | solution.py:483
  191.2 1.6 copy.22
  192.8 1.5 copy.23
  (1 shorter events, 0.0 us)

commit v2 on v1

v2 whole, which is shorter than its diff:
```python
import functools

import jax
import jax.numpy as jnp
from jax import lax
from jax.experimental import pallas as pl
from jax.experimental.pallas import tpu as pltpu
from jax.sharding import PartitionSpec as P

MULT = 16
SEG = 512
TILE = 128
ITERS = 4
NX = 4
NZ = 8
PER = 6
ZROWS = NX * PER
UNITS = 192
PLANE = NX * UNITS
ROWS = 32
CHUNK = NX * ROWS
PH = 3
MESH = pl.DeviceIdType.MESH
F32 = jnp.float32
BF16 = jnp.bfloat16


def dot(a, b):
    return jnp.dot(a, b, preferred_element_type=F32)


def kernel(
    n_grp,
    amp,
    pair_e,
    hole_e,
    pack_row,
    unpack_row,
    coef_index,
    table,
    tile_list,
    tile_count,
    w_hbm,
    l_hbm,
    slab_hbm,
    d_out,
    t_out,
    w,
    lint,
    slab,
    kron,
    slots,
    hole,
    perm,
    perm_t,
    pack,
    pack_t,
    doubles,
    ladder,
    packed,
    cols,
    panel,
    rows_in,
    half,
    cyc,
    slotted,
    back,
    own_rows,
    pick,
    picked,
    local_sem,
    slots_sem,
    forward_sem,
    row_sem,
    ring_sem,
    backward_sem,
    tx_sem,
    tg_sem,
):
    me = lax.axis_index("col")
    g = lax.axis_index("grp")
    z = me // NX
    x = me % NX

    def at_z(d):
        return (z + d + NZ) % NZ

    def at_x(d):
        return (x + d + NX) % NX

    def remote(src, dst, sems, index, grp, zz, xx):
        return pltpu.make_async_remote_copy(
            src_ref=src,
            dst_ref=dst,
            send_sem=sems.at[(0,) + index],
            recv_sem=sems.at[(1,) + index],
            device_id=(grp, zz * NX + xx),
            device_id_type=MESH,
        )

    others = [(dz, dx) for dz in (4, 3, 5, 2, 6, 1, 7, 0) for dx in (2, 1, 3, 0)][:-1]

    loads = [
        pltpu.make_async_copy(l_hbm, lint, local_sem.at[0]),
        pltpu.make_async_copy(w_hbm, w, local_sem.at[1]),
        pltpu.make_async_copy(slab_hbm, slab, local_sem.at[2]),
    ]
    for load in loads:
        load.start()

    barrier = pltpu.get_barrier_semaphore()
    for dz, dx in others:
        pl.semaphore_signal(
            barrier, inc=1, device_id=(g, at_z(dz) * NX + at_x(dx)), device_id_type=MESH
        )
    for d in range(1, n_grp):
        pl.semaphore_signal(
            barrier, inc=1, device_id=((g + d) % n_grp, me), device_id_type=MESH
        )

    def iota(shape, axis):
        return lax.broadcasted_iota(jnp.int32, shape, axis)

    def one_hot(match):
        return match.astype(F32).astype(BF16)

    def as_column(row):
        size = row.shape[1]
        eye = iota((size, size), 0) == iota((size, size), 1)
        return jnp.sum(jnp.where(eye, row, 0.0), axis=1, keepdims=True)

    pack_line = pack_row[...].astype(F32)
    lane_k = iota((UNITS, UNITS), 1)
    row_k = iota((UNITS, UNITS), 0)
    lane_k = (lane_k % 64) * 3 + lane_k // 64
    row_k = (row_k % 64) * 3 + row_k // 64
    pack[...] = one_hot(as_column(pack_line) == lane_k.astype(F32))
    for t in range(3):
        doubles[t * 64 : (t + 1) * 64, :] = amp[:, t * SEG : (t + 1) * SEG]

    pl.semaphore_wait(barrier, len(others) + (n_grp - 1))

    def slots_copy(d, to):
        return remote(
            unpack_row, slots.at[x if to else at_x(-d)], slots_sem, (d,), g, z, at_x(d)
        )

    def forward(dz, dx, to):
        zz, xx = at_z(dz), at_x(dx)
        place = cols.at[z, x] if to else cols.at[at_z(-dz), at_x(-dx)]
        return remote(packed.at[zz, xx], place, forward_sem, (dz, dx), g, zz, xx)

    def send_packed():
        value = dot(pack[...], doubles[...])
        for zz in range(NZ):
            for xx in range(NX):
                packed[zz, xx] = value[
                    zz * ZROWS : (zz + 1) * ZROWS, xx * TILE : (xx + 1) * TILE
                ].astype(BF16)
        for dz, dx in others:
            forward(dz, dx, True).start()
        cols[z, x] = packed[z, x]

    def ladder_part():
        for t in range(3):
            acc = None
            for k in range(3):
                part = dot(
                    doubles[k * 64 : (k + 1) * 64, :],
                    lint[k * SEG : (k + 1) * SEG, t * SEG : (t + 1) * SEG],
                )
                acc = part if acc is None else acc + part
            ladder[:, t * SEG : (t + 1) * SEG] = acc

    def row_copy(d, e, to):
        rows = pl.ds(pl.multiple_of(z * CHUNK, CHUNK), CHUNK)
        return remote(
            panel.at[e, rows, :],
            rows_in.at[x if to else at_x(-d), e],
            row_sem,
            (d, e),
            g,
            z,
            at_x(d),
        )

    def ring(way, step, e, to):
        sign = 1 if way == 0 else -1
        chunk = at_z(-sign * (step - 1)) if to else at_z(-sign * step)
        if step < 4:
            rows = pl.ds(pl.multiple_of(chunk * CHUNK, CHUNK), CHUNK)
        else:
            rows = pl.ds(pl.multiple_of(chunk * CHUNK + way * 64, 64), 64)
        ref = panel.at[e, rows, :]
        return remote(ref, ref, ring_sem, (way, step - 1, e), g, at_z(sign), x)

    def recouple(value, e):
        mixed = dot(value.astype(BF16), kron[e])
        return (value + (mixed[:, :TILE] + mixed[:, TILE:])).astype(BF16)

    def half_part(e):
        value = jnp.concatenate(
            [
                rows_in[xx, e, :, h * TILE : (h + 1) * TILE]
                for h in range(2)
                for xx in range(NX)
            ],
            axis=1,
        )
        half[e] = dot(value, w[e]).astype(BF16)

    def backward(dz, dx, to):
        zz, xx = at_z(dz), at_x(dx)
        place = back.at[z, x] if to else back.at[at_z(-dz), at_x(-dx)]
        return remote(slotted.at[zz, xx], place, backward_sem, (dz, dx), g, zz, xx)

    def own_copy(d, to):
        target = at_x(d)
        return remote(
            cyc.at[:, target],
            own_rows.at[x if to else at_x(-d)],
            tx_sem,
            (d,),
            g,
            z,
            target,
        )

    def group_copy(d, to):
        target = (g + d) % n_grp
        source = g if to else (g - d + n_grp) % n_grp
        return remote(pick.at[d], picked.at[source], tg_sem, (d,), target, z, x)

    for d in range(1, NX):
        slots_copy(d, True).start()
    send_packed()
    slots[x] = unpack_row[...]

    pack_t[...] = one_hot(pack_line == row_k.astype(F32))
    hole[...] = jnp.broadcast_to(as_column(hole_e[...]), hole.shape)

    def coef_step(k, acc):
        return jnp.where(coef_index[...] == k, table[k], acc)

    coefs = lax.fori_loop(
        0, table.shape[0], coef_step, jnp.zeros((PH, MULT, MULT), F32)
    )
    spread = one_hot(iota((TILE, MULT), 0) % MULT == iota((TILE, MULT), 1))
    same = iota((TILE, TILE), 0) // MULT == iota((TILE, TILE), 1) // MULT
    turned = (((1,), (1,)), ((), ()))
    for e in range(PH):
        high = coefs[e].astype(BF16)
        low = (coefs[e] - high.astype(F32)).astype(BF16)
        for i, part in enumerate((high, low)):
            tall = lax.dot_general(spread, part, turned, preferred_element_type=F32)
            full = lax.dot_general(
                tall.astype(BF16), spread, turned, preferred_element_type=F32
            )
            kron[e, :, i * TILE : (i + 1) * TILE] = jnp.where(same, full, 0.0).astype(
                BF16
            )

    for d in range(1, NX):
        slots_copy(d, False).wait_recv()
    raw = jnp.concatenate(
        [slots[xx] for xx in range(NX)] + [slots[xx] for xx in range(NX)], axis=0
    )
    raw = raw.astype(F32).astype(BF16)
    mine = iota((8, TILE), 0) == iota((8, TILE), 1) // ROWS
    owner = iota((1, TILE), 1) // ROWS
    for k in range(2 * PH):
        select = one_hot(
            iota((UNITS, TILE), 0) == (iota((UNITS, TILE), 1) % ROWS) * 2 * PH + k
        )
        found = jnp.where(mine, dot(raw, select), 0.0)
        unit = jnp.sum(found, axis=0, keepdims=True).astype(jnp.int32)
        line = (unit // PER) * ZROWS + unit % PER + owner * PER
        perm_t[:, k * TILE : (k + 1) * TILE] = one_hot(iota((PLANE, TILE), 0) == line)
        column = as_column(line.astype(F32)).astype(jnp.int32)
        perm[k * TILE : (k + 1) * TILE, :] = one_hot(iota((TILE, PLANE), 1) == column)

    loads[0].wait()

    def iteration(it, carry):
        @pl.when(it > 0)
        def _():
            send_packed()

        ladder_part()
        for dz, dx in reversed(others):
            forward(dz, dx, False).wait_recv()
        arrived = cols[...].reshape(PLANE, TILE)
        for e in range(PH):
            found = dot(perm[e * 256 : (e + 1) * 256, :], arrived)
            done = recouple(found, e)
            rows = pl.ds(pl.multiple_of(z * CHUNK, CHUNK), CHUNK)
            for h in range(2):
                lanes = slice(h * TILE, (h + 1) * TILE)
                panel[e, rows, lanes] = done[h * CHUNK : (h + 1) * CHUNK, :]
                rows_in[x, e, :, lanes] = done[h * CHUNK : (h + 1) * CHUNK, :]
            ring(0, 1, e, True).start()
            ring(1, 1, e, True).start()
            for d in (2, 1, 3):
                row_copy(d, e, True).start()
        for e in range(PH):
            for way in range(2):
                ring(way, 1, e, False).wait_recv()
                ring(way, 2, e, True).start()

        @pl.when(it == 0)
        def _():
            loads[1].wait()

        for e in range(PH):
            for way in range(2):
                ring(way, 2, e, False).wait_recv()
                ring(way, 3, e, True).start()
        for e in range(PH):
            for d in (1, 3, 2):
                row_copy(d, e, False).wait_recv()
            half_part(e)
            for way in range(2):
                ring(way, 3, e, False).wait_recv()
                ring(way, 4, e, True).start()
        value = None
        for e in range(PH):
            for way in range(2):
                ring(way, 4, e, False).wait_recv()
            block = dot(half[e], panel[e])
            for h in range(2):
                cyc[2 * e + h] = (
                    block[:, h * TILE : (h + 1) * TILE]
                    .reshape(NX, ROWS, TILE)
                    .astype(BF16)
                )
            part = dot(
                perm_t[:, e * 256 : (e + 1) * 256],
                cyc[2 * e : 2 * e + 2].reshape(256, TILE),
            )
            value = part if value is None else value + part
        slotted[...] = value.reshape(NZ, NX, ZROWS, TILE).astype(BF16)
        for dz, dx in others:
            backward(dz, dx, True).start()
        back[z, x] = slotted[z, x]

        @pl.when(it == ITERS - 1)
        def _():
            for d in (2, 1, 3):
                own_copy(d, True).start()
            own_rows[x] = cyc[:, x]
            for d in (1, 3, 2):
                own_copy(d, False).wait_recv()
            for d in range(n_grp):
                owner = (g + d) % n_grp
                count = jnp.int32(0)
                first = jnp.int32(0)
                second = jnp.int32(0)
                for s in range(tile_list.shape[1]):
                    tile = tile_list[owner, s]
                    mine = tile // 24 == g
                    local = tile - g * 24
                    blk = local % 8
                    where = (blk % 4) * (2 * PH) + (local // 8) * 2 + blk // 4
                    first = jnp.where(mine & (count == 0), where, first)
                    second = jnp.where(mine & (count == 1), where, second)
                    count = count + jnp.where(mine, 1, 0)
                flat = own_rows.reshape(NX * 2 * PH, ROWS, TILE)
                if d == 0:
                    picked[g, 0] = flat[first]
                    picked[g, 1] = flat[second]
                else:
                    pick[d, 0] = flat[first]
                    pick[d, 1] = flat[second]
                    group_copy(d, True).start()

        for dz, dx in reversed(others):
            backward(dz, dx, False).wait_recv()
        together = jnp.concatenate(
            [back[:, xx].reshape(UNITS, TILE) for xx in range(NX)], axis=1
        )
        returned = dot(pack_t[...], together)
        for t in range(3):
            lanes = slice(t * SEG, (t + 1) * SEG)
            total = (amp[:, lanes].astype(F32) + ladder[:, lanes]) + returned[
                t * 64 : (t + 1) * 64, :
            ]
            doubles[t * 64 : (t + 1) * 64, :] = (
                total / (pair_e[:, lanes] + hole[:, :1])
            ).astype(BF16)

        for dz, dx in others:
            forward(dz, dx, True).wait_send()
            backward(dz, dx, True).wait_send()
        for e in range(PH):
            for d in range(1, NX):
                row_copy(d, e, True).wait_send()
            for step in range(1, 5):
                for way in range(2):
                    ring(way, step, e, True).wait_send()
        return carry

    lax.fori_loop(0, ITERS, iteration, jnp.int32(0))

    for t in range(3):
        d_out[:, t * SEG : (t + 1) * SEG] = doubles[t * 64 : (t + 1) * 64, :]

    for d in range(1, n_grp):
        group_copy(d, False).wait_recv()
    loads[2].wait()
    live = tile_count[g]
    flat = picked.reshape(n_grp * 2, ROWS, TILE)
    parts = []
    for s in range(tile_list.shape[1]):
        group = tile_list[g, s] // 24
        rank = jnp.int32(0)
        for before in range(s):
            rank = rank + jnp.where(tile_list[g, before] // 24 == group, 1, 0)
        part = flat[group * 2 + jnp.minimum(rank, 1)]
        parts.append(
            (part.astype(F32) * jnp.where(s < live, 1.0, 0.0).astype(F32)).astype(BF16)
        )
    t_out[...] = dot(jnp.concatenate(parts, axis=1), slab[...]).astype(BF16)

    for d in range(1, NX):
        slots_copy(d, True).wait_send()
        own_copy(d, True).wait_send()
    for d in range(1, n_grp):
        group_copy(d, True).wait_send()


def body(
    amplitudes,
    ladder_int,
    pair_energy,
    hole_energy,
    pack_map,
    unpack_map,
    coupling_index,
    coupling_table,
    cycle_int,
    tile_list,
    tile_count,
    slabs,
):
    n_grp = lax.axis_size("grp")
    width_p = amplitudes.shape[2]
    width_r = cycle_int.shape[1]
    vmem = pl.BlockSpec(memory_space=pltpu.VMEM)
    smem = pl.BlockSpec(memory_space=pltpu.SMEM)
    anywhere = pl.BlockSpec(memory_space=pl.ANY)
    dma = pltpu.SemaphoreType.DMA
    doubles, triples = pl.pallas_call(
        functools.partial(kernel, n_grp),
        out_shape=(
            jax.ShapeDtypeStruct((64, width_p), BF16),
            jax.ShapeDtypeStruct((ROWS, width_r), BF16),
        ),
        in_specs=[vmem] * 6 + [smem] * 3 + [anywhere] * 3,
        out_specs=(vmem, vmem),
        scratch_shapes=[
            pltpu.VMEM((PH, width_r, width_r), BF16),
            pltpu.VMEM((width_p, width_p), BF16),
            pltpu.VMEM((width_r, width_r), BF16),
            pltpu.VMEM((PH, TILE, 2 * TILE), BF16),
            pltpu.VMEM((NX, 1, UNITS), jnp.int32),
            pltpu.VMEM((64, TILE), F32),
            pltpu.VMEM((PLANE, PLANE), BF16),
            pltpu.VMEM((PLANE, PLANE), BF16),
            pltpu.VMEM((UNITS, UNITS), BF16),
            pltpu.VMEM((UNITS, UNITS), BF16),
            pltpu.VMEM((UNITS, SEG), BF16),
            pltpu.VMEM((64, width_p), F32),
            pltpu.VMEM((NZ, NX, ZROWS, TILE), BF16),
            pltpu.VMEM((NZ, NX, ZROWS, TILE), BF16),
            pltpu.VMEM((PH, width_r, 2 * TILE), BF16),
            pltpu.VMEM((NX, PH, CHUNK, 2 * TILE), BF16),
            pltpu.VMEM((PH, CHUNK, width_r), BF16),
            pltpu.VMEM((2 * PH, NX, ROWS, TILE), BF16),
            pltpu.VMEM((NZ, NX, ZROWS, TILE), BF16),
            pltpu.VMEM((NZ, NX, ZROWS, TILE), BF16),
            pltpu.VMEM((NX, 2 * PH, ROWS, TILE), BF16),
            pltpu.VMEM((n_grp, 2, ROWS, TILE), BF16),
            pltpu.VMEM((n_grp, 2, ROWS, TILE), BF16),
            dma((3,)),
            dma((2, NX)),
            dma((2, NZ, NX)),
            dma((2, NX, PH)),
            dma((2, 2, 4, PH)),
            dma((2, NZ, NX)),
            dma((2, NX)),
            dma((2, n_grp)),
        ],
        compiler_params=pltpu.CompilerParams(
            collective_id=0, has_side_effects=True, vmem_limit_bytes=60 * 1024 * 1024
        ),
    )(
        amplitudes[0],
        pair_energy,
        hole_energy,
        pack_map.reshape(1, -1),
        unpack_map.reshape(1, -1),
        coupling_index,
        coupling_table,
        tile_list,
        tile_count,
        cycle_int,
        ladder_int[0],
        slabs.reshape(width_r, width_r),
    )
    return doubles[None], triples[None]


def solution(mesh):
    return jax.shard_map(
        body,
        mesh=mesh,
        in_specs=(
            P("grp", "col", None),
            P("grp", None, None),
            P("grp", None),
            P("grp", "col"),
            P("col"),
            P("col"),
            P("grp", None, None),
            P(),
            P("grp", None, None),
            P(),
            P(),
            P("grp", None, None, None),
        ),
        out_specs=(P("grp", "col", None), P("grp", "col", None)),
        check_vma=False,
    )
```

time: 195 us -> 159 us (0.82)
  Pallas kernels: 184 us -> 155 us
  local copies, waits for them, and re-layouts: 8.83 us -> 3.09 us
    pallas_call x1, Pallas kernels: 184 us -> 155 us  [body(): pl.pallas_call(functools.partial(kernel, n_grp), out_shape=(jax.ShapeDtyp...]
    reshape x2 -> x0, local copies, waits for them, and re-layouts: 2.79 us -> none  [the longest x1 1.43 us: body(): pack_map.reshape(-1, 1)]
where the time goes in v2:
time: 159 us
  Pallas kernels  155 us (97%)
  local copies, waits for them, and re-layouts  3.09 us (2%)
    pallas_call x1, Pallas kernels, body(): pl.pallas_call(functools.partial(kernel, n_grp), out_shape=(jax.ShapeDtyp...  155 us

profile of v2, /device:TPU:1, one launch (start us, length us, event | category | flops | bytes accessed | tf_op | source)
XLA Modules:
  0.0 158.6 jit_solution(509819995706249483)
XLA Ops:
  0.6 154.8 %shard_map.131 = (bf16[64,1536]{1,0:T(8,128)(2,1)}, bf16[32,1024]{1,0:T(8,128)(2,1)}) custom-call(bf16[64,1536]{1,0:T(8,128)(2,1)} %bitcast.10, f32[1,1536]{1,0:T(1,128)} %pair_e.1, f32[1,64]{1,0:T(1,128)} %hole_e.1, s32[1,192]{1,0:T(1,128)} %bitcast.12, s32[1,192]{1,0:T(1,128)} %bitcast.13, s32[3,16,16]{2,1,0:T(8,128)} %coef_index.1, f32[64]{0:T(128)} %table.1, ...), custom_call_target="tpu_custom_call" | custom-call | tf_op jit(solution)/shard_map/pallas_call | solution.py:452
  155.5 1.6 %copy.16 = bf16[1,64,1536]{2,1,0:T(8,128)(2,1)} copy(bf16[1,64,1536]{2,1,0:T(8,128)(2,1)} %bitcast.9) | data formatting | bytes 393216
  157.1 1.5 copy.17

commit v3 on v2

--- a/solution.py
+++ b/solution.py
@@ -50,30 +50,39 @@
     slab,
     kron,
     slots,
-    hole,
     perm,
     perm_t,
     pack,
     pack_t,
     doubles,
     ladder,
-    packed,
-    cols,
+    amp_out,
+    amp_in,
+    mark_out,
+    mark_in,
+    ladder_out,
+    ladder_in,
+    slotted,
+    back,
+    current,
+    start,
+    source,
+    denom,
     panel,
     rows_in,
     half,
     cyc,
-    slotted,
-    back,
     own_rows,
     pick,
     picked,
     local_sem,
     slots_sem,
-    forward_sem,
+    amp_sem,
+    mark_sem,
+    ladder_sem,
+    back_sem,
     row_sem,
     ring_sem,
-    backward_sem,
     tx_sem,
     tg_sem,
 ):
@@ -145,63 +154,94 @@
             unpack_row, slots.at[x if to else at_x(-d)], slots_sem, (d,), g, z, at_x(d)
         )
 
-    def forward(dz, dx, to):
+    def exchange(src, dst, sems, dz, dx, to):
         zz, xx = at_z(dz), at_x(dx)
-        place = cols.at[z, x] if to else cols.at[at_z(-dz), at_x(-dx)]
-        return remote(packed.at[zz, xx], place, forward_sem, (dz, dx), g, zz, xx)
-
-    def send_packed():
-        value = dot(pack[...], doubles[...])
+        place = dst.at[z, x] if to else dst.at[at_z(-dz), at_x(-dx)]
+        return remote(src.at[zz, xx], place, sems, (dz, dx), g, zz, xx)
+
+    def start_all(src, dst, sems):
+        for dz, dx in others:
+            exchange(src, dst, sems, dz, dx, True).start()
+        dst[z, x] = src[z, x]
+
+    def receive_all(src, dst, sems):
+        for dz, dx in reversed(others):
+            exchange(src, dst, sems, dz, dx, False).wait_recv()
+
+    def sent_all(src, dst, sems):
+        for dz, dx in others:
+            exchange(src, dst, sems, dz, dx, True).wait_send()
+
+    def pack_into(dst, value):
         for zz in range(NZ):
             for xx in range(NX):
-                packed[zz, xx] = value[
+                dst[zz, xx] = value[
                     zz * ZROWS : (zz + 1) * ZROWS, xx * TILE : (xx + 1) * TILE
                 ].astype(BF16)
-        for dz, dx in others:
-            forward(dz, dx, True).start()
-        cols[z, x] = packed[z, x]
-
-    def ladder_part():
-        for t in range(3):
-            acc = None
-            for k in range(3):
-                part = dot(
-                    doubles[k * 64 : (k + 1) * 64, :],
-                    lint[k * SEG : (k + 1) * SEG, t * SEG : (t + 1) * SEG],
-                )
-                acc = part if acc is None else acc + part
-            ladder[:, t * SEG : (t + 1) * SEG] = acc
-
-    def row_copy(d, e, to):
+
+    def ladder_part(t):
+        acc = None
+        for k in range(3):
+            part = dot(
+                doubles[k * 64 : (k + 1) * 64, :],
+                lint[k * SEG : (k + 1) * SEG, t * SEG : (t + 1) * SEG],
+            )
+            acc = part if acc is None else acc + part
+        ladder[t * 64 : (t + 1) * 64, :] = acc.astype(BF16)
+
+    def send_ladder():
+        pack_into(ladder_out, dot(pack[...], ladder[...]))
+        start_all(ladder_out, ladder_in, ladder_sem)
+
+    def row_copy(par, d, e, to):
         rows = pl.ds(pl.multiple_of(z * CHUNK, CHUNK), CHUNK)
         return remote(
-            panel.at[e, rows, :],
-            rows_in.at[x if to else at_x(-d), e],
+            panel.at[par, e, rows, :],
+            rows_in.at[par, x if to else at_x(-d), e],
             row_sem,
-            (d, e),
+            (par, d, e),
             g,
             z,
             at_x(d),
         )
 
-    def ring(way, step, e, to):
+    def ring(par, way, step, e, to):
         sign = 1 if way == 0 else -1
         chunk = at_z(-sign * (step - 1)) if to else at_z(-sign * step)
         if step < 4:
             rows = pl.ds(pl.multiple_of(chunk * CHUNK, CHUNK), CHUNK)
         else:
             rows = pl.ds(pl.multiple_of(chunk * CHUNK + way * 64, 64), 64)
-        ref = panel.at[e, rows, :]
-        return remote(ref, ref, ring_sem, (way, step - 1, e), g, at_z(sign), x)
+        ref = panel.at[par, e, rows, :]
+        return remote(
+            ref, ref, ring_sem, (par, way, step - 1, e), g, at_z(sign), x
+        )
+
+    def pass_on(par, step, e):
+        for way in range(2):
+            ring(par, way, step, e, False).wait_recv()
+            ring(par, way, step + 1, e, True).start()
 
     def recouple(value, e):
         mixed = dot(value.astype(BF16), kron[e])
         return (value + (mixed[:, :TILE] + mixed[:, TILE:])).astype(BF16)
 
-    def half_part(e):
+    def launch(par, e):
+        done = recouple(current[e * 256 : (e + 1) * 256, :].astype(F32), e)
+        rows = pl.ds(pl.multiple_of(z * CHUNK, CHUNK), CHUNK)
+        for h in range(2):
+            lanes = slice(h * TILE, (h + 1) * TILE)
+            panel[par, e, rows, lanes] = done[h * CHUNK : (h + 1) * CHUNK, :]
+            rows_in[par, x, e, :, lanes] = done[h * CHUNK : (h + 1) * CHUNK, :]
+        ring(par, 0, 1, e, True).start()
+        ring(par, 1, 1, e, True).start()
+        for d in (2, 1, 3):
+            row_copy(par, d, e, True).start()
+
+    def half_part(par, e):
         value = jnp.concatenate(
             [
-                rows_in[xx, e, :, h * TILE : (h + 1) * TILE]
+                rows_in[par, xx, e, :, h * TILE : (h + 1) * TILE]
                 for h in range(2)
                 for xx in range(NX)
             ],
@@ -209,10 +249,11 @@
         )
         half[e] = dot(value, w[e]).astype(BF16)
 
-    def backward(dz, dx, to):
-        zz, xx = at_z(dz), at_x(dx)
-        place = back.at[z, x] if to else back.at[at_z(-dz), at_x(-dx)]
-        return remote(slotted.at[zz, xx], place, backward_sem, (dz, dx), g, zz, xx)
+    def unpacked():
+        together = jnp.concatenate(
+            [back[:, xx].reshape(UNITS, TILE) for xx in range(NX)], axis=1
+        )
+        return dot(pack_t[...], together).astype(BF16)
 
     def own_copy(d, to):
         target = at_x(d)
@@ -233,11 +274,11 @@
 
     for d in range(1, NX):
         slots_copy(d, True).start()
-    send_packed()
+    pack_into(amp_out, dot(pack[...], doubles[...]))
+    start_all(amp_out, amp_in, amp_sem)
     slots[x] = unpack_row[...]
 
     pack_t[...] = one_hot(pack_line == row_k.astype(F32))
-    hole[...] = jnp.broadcast_to(as_column(hole_e[...]), hole.shape)
 
     def coef_step(k, acc):
         return jnp.where(coef_index[...] == k, table[k], acc)
@@ -279,130 +320,149 @@
         column = as_column(line.astype(F32)).astype(jnp.int32)
         perm[k * TILE : (k + 1) * TILE, :] = one_hot(iota((TILE, PLANE), 1) == column)
 
+    receive_all(amp_out, amp_in, amp_sem)
+    found = dot(perm[...], amp_in[...].reshape(PLANE, TILE)).astype(BF16)
+    current[...] = found
+    start[...] = found
+    for e in range(PH):
+        launch(0, e)
+
     loads[0].wait()
+    for t in range(3):
+        ladder_part(t)
+    send_ladder()
+
+    hole = as_column(hole_e[...])
+    hole_a = hole.astype(BF16).astype(F32)
+    hole_b = (hole - hole_a).astype(BF16).astype(F32)
+    hole_c = hole - hole_a - hole_b
+    lane = iota((64, TILE), 1)
+    marks = []
+    for t in range(3):
+        mark = jnp.where(lane == 3 + t, 1.0, 0.0)
+        mark = jnp.where(lane == 0, hole_a, mark)
+        mark = jnp.where(lane == 1, hole_b, mark)
+        mark = jnp.where(lane == 2, hole_c, mark)
+        marks.append(mark.astype(BF16))
+    marked = dot(pack[...], jnp.concatenate(marks, axis=0))
+    for zz in range(NZ):
+        line = marked[zz * ZROWS : (zz + 1) * ZROWS, :].astype(BF16)
+        for xx in range(NX):
+            mark_out[zz, xx] = line
+    start_all(mark_out, mark_in, mark_sem)
+    for e in range(PH):
+        pass_on(0, 1, e)
+    loads[1].wait()
+    receive_all(mark_out, mark_in, mark_sem)
+    marked = dot(perm[...], mark_in[...].reshape(PLANE, TILE))
+    pairs = jnp.zeros((PLANE, TILE), F32)
+    for t in range(3):
+        lanes = pl.ds(pl.multiple_of(t * SEG + x * TILE, TILE), TILE)
+        pairs = pairs + marked[:, 3 + t : 4 + t] * pair_e[:, lanes]
+    denom[...] = pairs + (marked[:, 0:1] + marked[:, 1:2] + marked[:, 2:3])
 
     def iteration(it, carry):
+        par = it % 2
+
         @pl.when(it > 0)
         def _():
-            send_packed()
-
-        ladder_part()
-        for dz, dx in reversed(others):
-            forward(dz, dx, False).wait_recv()
-        arrived = cols[...].reshape(PLANE, TILE)
+            for e in range(PH):
+                pass_on(par, 1, e)
+
         for e in range(PH):
-            found = dot(perm[e * 256 : (e + 1) * 256, :], arrived)
-            done = recouple(found, e)
-            rows = pl.ds(pl.multiple_of(z * CHUNK, CHUNK), CHUNK)
-            for h in range(2):
-                lanes = slice(h * TILE, (h + 1) * TILE)
-                panel[e, rows, lanes] = done[h * CHUNK : (h + 1) * CHUNK, :]
-                rows_in[x, e, :, lanes] = done[h * CHUNK : (h + 1) * CHUNK, :]
-            ring(0, 1, e, True).start()
-            ring(1, 1, e, True).start()
-            for d in (2, 1, 3):
-                row_copy(d, e, True).start()
+            for d in (1, 3, 2):
+                row_copy(par, d, e, False).wait_recv()
+            half_part(par, e)
+            pass_on(par, 2, e)
+
+        @pl.when(it > 0)
+        def _():
+            receive_all(slotted, back, back_sem)
+            doubles[...] = unpacked()
+
+        for e in range(PH):
+
+            @pl.when(it > 0)
+            def _():
+                ladder_part(e)
+
+            pass_on(par, 3, e)
+
+        @pl.when(it > 0)
+        def _():
+            send_ladder()
+            sent_all(slotted, back, back_sem)
+
+        receive_all(ladder_out, ladder_in, ladder_sem)
+        source[...] = dot(perm[...], ladder_in[...].reshape(PLANE, TILE)) + start[
+            ...
+        ].astype(F32)
         for e in range(PH):
             for way in range(2):
-                ring(way, 1, e, False).wait_recv()
-                ring(way, 2, e, True).start()
-
-        @pl.when(it == 0)
-        def _():
-            loads[1].wait()
-
-        for e in range(PH):
-            for way in range(2):
-                ring(way, 2, e, False).wait_recv()
-                ring(way, 3, e, True).start()
-        for e in range(PH):
-            for d in (1, 3, 2):
-                row_copy(d, e, False).wait_recv()
-            half_part(e)
-            for way in range(2):
-                ring(way, 3, e, False).wait_recv()
-                ring(way, 4, e, True).start()
-        value = None
-        for e in range(PH):
-            for way in range(2):
-                ring(way, 4, e, False).wait_recv()
-            block = dot(half[e], panel[e])
+                ring(par, way, 4, e, False).wait_recv()
+            block = dot(half[e], panel[par, e])
             for h in range(2):
-                cyc[2 * e + h] = (
-                    block[:, h * TILE : (h + 1) * TILE]
-                    .reshape(NX, ROWS, TILE)
-                    .astype(BF16)
-                )
-            part = dot(
-                perm_t[:, e * 256 : (e + 1) * 256],
-                cyc[2 * e : 2 * e + 2].reshape(256, TILE),
-            )
-            value = part if value is None else value + part
-        slotted[...] = value.reshape(NZ, NX, ZROWS, TILE).astype(BF16)
-        for dz, dx in others:
-            backward(dz, dx, True).start()
-        back[z, x] = slotted[z, x]
+                done = block[:, h * TILE : (h + 1) * TILE].astype(BF16)
+                cyc[2 * e + h] = done.reshape(NX, ROWS, TILE)
+                rows = slice((2 * e + h) * CHUNK, (2 * e + h + 1) * CHUNK)
+                current[rows, :] = (
+                    (source[rows, :] + done.astype(F32)) / denom[rows, :]
+                ).astype(BF16)
+
+            @pl.when(it < ITERS - 1)
+            def _():
+                launch((it + 1) % 2, e)
 
         @pl.when(it == ITERS - 1)
         def _():
             for d in (2, 1, 3):
                 own_copy(d, True).start()
-            own_rows[x] = cyc[:, x]
-            for d in (1, 3, 2):
-                own_copy(d, False).wait_recv()
-            for d in range(n_grp):
-                owner = (g + d) % n_grp
-                count = jnp.int32(0)
-                first = jnp.int32(0)
-                second = jnp.int32(0)
-                for s in range(tile_list.shape[1]):
-                    tile = tile_list[owner, s]
-                    mine = tile // 24 == g
-                    local = tile - g * 24
-                    blk = local % 8
-                    where = (blk % 4) * (2 * PH) + (local // 8) * 2 + blk // 4
-                    first = jnp.where(mine & (count == 0), where, first)
-                    second = jnp.where(mine & (count == 1), where, second)
-                    count = count + jnp.where(mine, 1, 0)
-                flat = own_rows.reshape(NX * 2 * PH, ROWS, TILE)
-                if d == 0:
-                    picked[g, 0] = flat[first]
-                    picked[g, 1] = flat[second]
-                else:
-                    pick[d, 0] = flat[first]
-                    pick[d, 1] = flat[second]
-                    group_copy(d, True).start()
-
-        for dz, dx in reversed(others):
-            backward(dz, dx, False).wait_recv()
-        together = jnp.concatenate(
-            [back[:, xx].reshape(UNITS, TILE) for xx in range(NX)], axis=1
-        )
-        returned = dot(pack_t[...], together)
-        for t in range(3):
-            lanes = slice(t * SEG, (t + 1) * SEG)
-            total = (amp[:, lanes].astype(F32) + ladder[:, lanes]) + returned[
-                t * 64 : (t + 1) * 64, :
-            ]
-            doubles[t * 64 : (t + 1) * 64, :] = (
-                total / (pair_e[:, lanes] + hole[:, :1])
-            ).astype(BF16)
-
-        for dz, dx in others:
-            forward(dz, dx, True).wait_send()
-            backward(dz, dx, True).wait_send()
+
+        slotted[...] = (
+            dot(perm_t[...], current[...]).reshape(NZ, NX, ZROWS, TILE).astype(BF16)
+        )
+        start_all(slotted, back, back_sem)
+        sent_all(ladder_out, ladder_in, ladder_sem)
         for e in range(PH):
             for d in range(1, NX):
-                row_copy(d, e, True).wait_send()
+                row_copy(par, d, e, True).wait_send()
             for step in range(1, 5):
                 for way in range(2):
-                    ring(way, step, e, True).wait_send()
+                    ring(par, way, step, e, True).wait_send()
         return carry
 
     lax.fori_loop(0, ITERS, iteration, jnp.int32(0))
 
+    own_rows[x] = cyc[:, x]
+    for d in (1, 3, 2):
+        own_copy(d, False).wait_recv()
+    for d in range(n_grp):
+        owner = (g + d) % n_grp
+        count = jnp.int32(0)
+        first = jnp.int32(0)
+        second = jnp.int32(0)
+        for s in range(tile_list.shape[1]):
+            tile = tile_list[owner, s]
+            mine = tile // 24 == g
+            local = tile - g * 24
+            blk = local % 8
+            where = (blk % 4) * (2 * PH) + (local // 8) * 2 + blk // 4
+            first = jnp.where(mine & (count == 0), where, first)
+            second = jnp.where(mine & (count == 1), where, second)
+            count = count + jnp.where(mine, 1, 0)
+        flat = own_rows.reshape(NX * 2 * PH, ROWS, TILE)
+        if d == 0:
+            picked[g, 0] = flat[first]
+            picked[g, 1] = flat[second]
+        else:
+            pick[d, 0] = flat[first]
+            pick[d, 1] = flat[second]
+            group_copy(d, True).start()
+
+    receive_all(slotted, back, back_sem)
+    final = unpacked()
     for t in range(3):
-        d_out[:, t * SEG : (t + 1) * SEG] = doubles[t * 64 : (t + 1) * 64, :]
+        d_out[:, t * SEG : (t + 1) * SEG] = final[t * 64 : (t + 1) * 64, :]
 
     for d in range(1, n_grp):
         group_copy(d, False).wait_recv()
@@ -426,6 +486,9 @@
         own_copy(d, True).wait_send()
     for d in range(1, n_grp):
         group_copy(d, True).wait_send()
+    sent_all(amp_out, amp_in, amp_sem)
+    sent_all(mark_out, mark_in, mark_sem)
+    sent_all(slotted, back, back_sem)
 
 
 def body(
@@ -463,30 +526,34 @@
             pltpu.VMEM((width_r, width_r), BF16),
             pltpu.VMEM((PH, TILE, 2 * TILE), BF16),
             pltpu.VMEM((NX, 1, UNITS), jnp.int32),
-            pltpu.VMEM((64, TILE), F32),
             pltpu.VMEM((PLANE, PLANE), BF16),
             pltpu.VMEM((PLANE, PLANE), BF16),
             pltpu.VMEM((UNITS, UNITS), BF16),
             pltpu.VMEM((UNITS, UNITS), BF16),
             pltpu.VMEM((UNITS, SEG), BF16),
-            pltpu.VMEM((64, width_p), F32),
-            pltpu.VMEM((NZ, NX, ZROWS, TILE), BF16),
-            pltpu.VMEM((NZ, NX, ZROWS, TILE), BF16),
-            pltpu.VMEM((PH, width_r, 2 * TILE), BF16),
-            pltpu.VMEM((NX, PH, CHUNK, 2 * TILE), BF16),
+            pltpu.VMEM((UNITS, SEG), BF16),
+        ]
+        + [pltpu.VMEM((NZ, NX, ZROWS, TILE), BF16)] * 8
+        + [
+            pltpu.VMEM((PLANE, TILE), BF16),
+            pltpu.VMEM((PLANE, TILE), BF16),
+            pltpu.VMEM((PLANE, TILE), F32),
+            pltpu.VMEM((PLANE, TILE), F32),
+            pltpu.VMEM((2, PH, width_r, 2 * TILE), BF16),
+            pltpu.VMEM((2, NX, PH, CHUNK, 2 * TILE), BF16),
             pltpu.VMEM((PH, CHUNK, width_r), BF16),
             pltpu.VMEM((2 * PH, NX, ROWS, TILE), BF16),
-            pltpu.VMEM((NZ, NX, ZROWS, TILE), BF16),
-            pltpu.VMEM((NZ, NX, ZROWS, TILE), BF16),
             pltpu.VMEM((NX, 2 * PH, ROWS, TILE), BF16),
             pltpu.VMEM((n_grp, 2, ROWS, TILE), BF16),
             pltpu.VMEM((n_grp, 2, ROWS, TILE), BF16),
             dma((3,)),
             dma((2, NX)),
             dma((2, NZ, NX)),
-            dma((2, NX, PH)),
-            dma((2, 2, 4, PH)),
             dma((2, NZ, NX)),
+            dma((2, NZ, NX)),
+            dma((2, NZ, NX)),
+            dma((2, 2, NX, PH)),
+            dma((2, 2, 2, 4, PH)),
             dma((2, NX)),
             dma((2, n_grp)),
         ],

time: 159 us -> 146 us (0.918)
  Pallas kernels: 155 us -> 142 us
    pallas_call x1, Pallas kernels: 155 us -> 142 us  [body(): pl.pallas_call(functools.partial(kernel, n_grp), out_shape=(jax.ShapeDtyp...]
where the time goes in v3:
time: 146 us
  Pallas kernels  142 us (97%)
  local copies, waits for them, and re-layouts  3.09 us (2%)
    pallas_call x1, Pallas kernels, body(): pl.pallas_call(functools.partial(kernel, n_grp), out_shape=(jax.ShapeDtyp...  142 us
    unnamed x2, local copies, waits for them, and re-layouts  3.09 us

profile of v3, /device:TPU:1, one launch (start us, length us, event | category | flops | bytes accessed | tf_op | source)
XLA Modules:
  0.0 145.9 jit_solution(4247378682495775477)
XLA Ops:
  0.6 142.2 %shard_map.131 = (bf16[64,1536]{1,0:T(8,128)(2,1)}, bf16[32,1024]{1,0:T(8,128)(2,1)}) custom-call(bf16[64,1536]{1,0:T(8,128)(2,1)} %bitcast.10, f32[1,1536]{1,0:T(1,128)} %pair_e.1, f32[1,64]{1,0:T(1,128)} %hole_e.1, s32[1,192]{1,0:T(1,128)} %bitcast.12, s32[1,192]{1,0:T(1,128)} %bitcast.13, s32[3,16,16]{2,1,0:T(8,128)} %coef_index.1, f32[64]{0:T(128)} %table.1, ...), custom_call_target="tpu_custom_call" | custom-call | tf_op jit(solution)/shard_map/pallas_call | solution.py:515
  142.8 1.6 %copy.16 = bf16[1,64,1536]{2,1,0:T(8,128)(2,1)} copy(bf16[1,64,1536]{2,1,0:T(8,128)(2,1)} %bitcast.9) | data formatting | bytes 393216
  144.4 1.5 %copy.17 = bf16[1,32,1024]{2,1,0:T(8,128)(2,1)} copy(bf16[1,32,1024]{2,1,0:T(8,128)(2,1)} %bitcast.11) | data formatting | bytes 131072

commit v4 on v3

--- a/solution.py
+++ b/solution.py
@@ -278,55 +278,6 @@
     start_all(amp_out, amp_in, amp_sem)
     slots[x] = unpack_row[...]
 
-    pack_t[...] = one_hot(pack_line == row_k.astype(F32))
-
-    def coef_step(k, acc):
-        return jnp.where(coef_index[...] == k, table[k], acc)
-
-    coefs = lax.fori_loop(
-        0, table.shape[0], coef_step, jnp.zeros((PH, MULT, MULT), F32)
-    )
-    spread = one_hot(iota((TILE, MULT), 0) % MULT == iota((TILE, MULT), 1))
-    same = iota((TILE, TILE), 0) // MULT == iota((TILE, TILE), 1) // MULT
-    turned = (((1,), (1,)), ((), ()))
-    for e in range(PH):
-        high = coefs[e].astype(BF16)
-        low = (coefs[e] - high.astype(F32)).astype(BF16)
-        for i, part in enumerate((high, low)):
-            tall = lax.dot_general(spread, part, turned, preferred_element_type=F32)
-            full = lax.dot_general(
-                tall.astype(BF16), spread, turned, preferred_element_type=F32
-            )
-            kron[e, :, i * TILE : (i + 1) * TILE] = jnp.where(same, full, 0.0).astype(
-                BF16
-            )
-
-    for d in range(1, NX):
-        slots_copy(d, False).wait_recv()
-    raw = jnp.concatenate(
-        [slots[xx] for xx in range(NX)] + [slots[xx] for xx in range(NX)], axis=0
-    )
-    raw = raw.astype(F32).astype(BF16)
-    mine = iota((8, TILE), 0) == iota((8, TILE), 1) // ROWS
-    owner = iota((1, TILE), 1) // ROWS
-    for k in range(2 * PH):
-        select = one_hot(
-            iota((UNITS, TILE), 0) == (iota((UNITS, TILE), 1) % ROWS) * 2 * PH + k
-        )
-        found = jnp.where(mine, dot(raw, select), 0.0)
-        unit = jnp.sum(found, axis=0, keepdims=True).astype(jnp.int32)
-        line = (unit // PER) * ZROWS + unit % PER + owner * PER
-        perm_t[:, k * TILE : (k + 1) * TILE] = one_hot(iota((PLANE, TILE), 0) == line)
-        column = as_column(line.astype(F32)).astype(jnp.int32)
-        perm[k * TILE : (k + 1) * TILE, :] = one_hot(iota((TILE, PLANE), 1) == column)
-
-    receive_all(amp_out, amp_in, amp_sem)
-    found = dot(perm[...], amp_in[...].reshape(PLANE, TILE)).astype(BF16)
-    current[...] = found
-    start[...] = found
-    for e in range(PH):
-        launch(0, e)
-
     loads[0].wait()
     for t in range(3):
         ladder_part(t)
@@ -350,53 +301,112 @@
         for xx in range(NX):
             mark_out[zz, xx] = line
     start_all(mark_out, mark_in, mark_sem)
+    pack_t[...] = one_hot(pack_line == row_k.astype(F32))
+
+    def coef_step(k, acc):
+        return jnp.where(coef_index[...] == k, table[k], acc)
+
+    coefs = lax.fori_loop(
+        0, table.shape[0], coef_step, jnp.zeros((PH, MULT, MULT), F32)
+    )
+    spread = one_hot(iota((TILE, MULT), 0) % MULT == iota((TILE, MULT), 1))
+    same = iota((TILE, TILE), 0) // MULT == iota((TILE, TILE), 1) // MULT
+    turned = (((1,), (1,)), ((), ()))
     for e in range(PH):
-        pass_on(0, 1, e)
-    loads[1].wait()
-    receive_all(mark_out, mark_in, mark_sem)
-    marked = dot(perm[...], mark_in[...].reshape(PLANE, TILE))
-    pairs = jnp.zeros((PLANE, TILE), F32)
-    for t in range(3):
-        lanes = pl.ds(pl.multiple_of(t * SEG + x * TILE, TILE), TILE)
-        pairs = pairs + marked[:, 3 + t : 4 + t] * pair_e[:, lanes]
-    denom[...] = pairs + (marked[:, 0:1] + marked[:, 1:2] + marked[:, 2:3])
+        high = coefs[e].astype(BF16)
+        low = (coefs[e] - high.astype(F32)).astype(BF16)
+        for i, part in enumerate((high, low)):
+            tall = lax.dot_general(spread, part, turned, preferred_element_type=F32)
+            full = lax.dot_general(
+                tall.astype(BF16), spread, turned, preferred_element_type=F32
+            )
+            kron[e, :, i * TILE : (i + 1) * TILE] = jnp.where(same, full, 0.0).astype(
+                BF16
+            )
+
+    for d in range(1, NX):
+        slots_copy(d, False).wait_recv()
+    raw = jnp.concatenate(
+        [slots[xx] for xx in range(NX)] + [slots[xx] for xx in range(NX)], axis=0
+    )
+    raw = raw.astype(F32).astype(BF16)
+    mine = iota((8, TILE), 0) == iota((8, TILE), 1) // ROWS
+    owner = iota((1, TILE), 1) // ROWS
+    for k in range(2 * PH):
+        select = one_hot(
+            iota((UNITS, TILE), 0) == (iota((UNITS, TILE), 1) % ROWS) * 2 * PH + k
+        )
+        found = jnp.where(mine, dot(raw, select), 0.0)
+        unit = jnp.sum(found, axis=0, keepdims=True).astype(jnp.int32)
+        line = (unit // PER) * ZROWS + unit % PER + owner * PER
+        perm_t[:, k * TILE : (k + 1) * TILE] = one_hot(iota((PLANE, TILE), 0) == line)
+        column = as_column(line.astype(F32)).astype(jnp.int32)
+        perm[k * TILE : (k + 1) * TILE, :] = one_hot(iota((TILE, PLANE), 1) == column)
+
+    receive_all(amp_out, amp_in, amp_sem)
+    found = dot(perm[...], amp_in[...].reshape(PLANE, TILE)).astype(BF16)
+    current[...] = found
+    start[...] = found
+    for e in range(PH):
+        launch(0, e)
 
     def iteration(it, carry):
         par = it % 2
 
-        @pl.when(it > 0)
+        for e in range(PH):
+            pass_on(par, 1, e)
+
+        @pl.when(it == 0)
         def _():
-            for e in range(PH):
-                pass_on(par, 1, e)
+            loads[1].wait()
 
         for e in range(PH):
             for d in (1, 3, 2):
                 row_copy(par, d, e, False).wait_recv()
             half_part(par, e)
-            pass_on(par, 2, e)
+
+        @pl.when(it == 0)
+        def _():
+            receive_all(mark_out, mark_in, mark_sem)
+            marked = dot(perm[...], mark_in[...].reshape(PLANE, TILE))
+            pairs = jnp.zeros((PLANE, TILE), F32)
+            for t in range(3):
+                lanes = pl.ds(pl.multiple_of(t * SEG + x * TILE, TILE), TILE)
+                pairs = pairs + marked[:, 3 + t : 4 + t] * pair_e[:, lanes]
+            denom[...] = pairs + (marked[:, 0:1] + marked[:, 1:2] + marked[:, 2:3])
 
         @pl.when(it > 0)
         def _():
             receive_all(slotted, back, back_sem)
             doubles[...] = unpacked()
-
-        for e in range(PH):
-
-            @pl.when(it > 0)
-            def _():
-                ladder_part(e)
-
-            pass_on(par, 3, e)
+            ladder_part(0)
+
+        pass_on(par, 2, 0)
 
         @pl.when(it > 0)
         def _():
+            ladder_part(1)
+
+        pass_on(par, 2, 1)
+
+        @pl.when(it > 0)
+        def _():
+            ladder_part(2)
             send_ladder()
+
+        pass_on(par, 2, 2)
+
+        @pl.when(it > 0)
+        def _():
             sent_all(slotted, back, back_sem)
 
+        for e in range(PH):
+            pass_on(par, 3, e)
         receive_all(ladder_out, ladder_in, ladder_sem)
         source[...] = dot(perm[...], ladder_in[...].reshape(PLANE, TILE)) + start[
             ...
         ].astype(F32)
+        value = None
         for e in range(PH):
             for way in range(2):
                 ring(par, way, 4, e, False).wait_recv()
@@ -409,6 +419,15 @@
                     (source[rows, :] + done.astype(F32)) / denom[rows, :]
                 ).astype(BF16)
 
+            part = dot(
+                perm_t[:, e * 256 : (e + 1) * 256],
+                current[e * 256 : (e + 1) * 256, :],
+            )
+            value = part if value is None else value + part
+            if e == PH - 1:
+                slotted[...] = value.reshape(NZ, NX, ZROWS, TILE).astype(BF16)
+                start_all(slotted, back, back_sem)
+
             @pl.when(it < ITERS - 1)
             def _():
                 launch((it + 1) % 2, e)
@@ -418,10 +437,6 @@
             for d in (2, 1, 3):
                 own_copy(d, True).start()
 
-        slotted[...] = (
-            dot(perm_t[...], current[...]).reshape(NZ, NX, ZROWS, TILE).astype(BF16)
-        )
-        start_all(slotted, back, back_sem)
         sent_all(ladder_out, ladder_in, ladder_sem)
         for e in range(PH):
             for d in range(1, NX):

time: 146 us -> 135 us (0.925)
  Pallas kernels: 142 us -> 131 us
    pallas_call x1, Pallas kernels: 142 us -> 131 us  [body(): pl.pallas_call(functools.partial(kernel, n_grp), out_shape=(jax.ShapeDtyp...]
where the time goes in v4:
time: 135 us
  Pallas kernels  131 us (97%)
  local copies, waits for them, and re-layouts  3.09 us (2%)
    pallas_call x1, Pallas kernels, body(): pl.pallas_call(functools.partial(kernel, n_grp), out_shape=(jax.ShapeDtyp...  131 us
    unnamed x2, local copies, waits for them, and re-layouts  3.09 us

profile of v4, /device:TPU:1, one launch (start us, length us, event | category | flops | bytes accessed | tf_op | source)
XLA Modules:
  0.0 135.1 jit_solution(6534076013442798210)
XLA Ops:
  0.6 131.4 %shard_map.131 = (bf16[64,1536]{1,0:T(8,128)(2,1)}, bf16[32,1024]{1,0:T(8,128)(2,1)}) custom-call(bf16[64,1536]{1,0:T(8,128)(2,1)} %bitcast.10, f32[1,1536]{1,0:T(1,128)} %pair_e.1, f32[1,64]{1,0:T(1,128)} %hole_e.1, s32[1,192]{1,0:T(1,128)} %bitcast.12, s32[1,192]{1,0:T(1,128)} %bitcast.13, s32[3,16,16]{2,1,0:T(8,128)} %coef_index.1, f32[64]{0:T(128)} %table.1, ...), custom_call_target="tpu_custom_call" | custom-call | tf_op jit(solution)/shard_map/pallas_call | solution.py:530
  132.0 1.6 %copy.16 = bf16[1,64,1536]{2,1,0:T(8,128)(2,1)} copy(bf16[1,64,1536]{2,1,0:T(8,128)(2,1)} %bitcast.9) | data formatting | bytes 393216
  133.7 1.5 %copy.17 = bf16[1,32,1024]{2,1,0:T(8,128)(2,1)} copy(bf16[1,32,1024]{2,1,0:T(8,128)(2,1)} %bitcast.11) | data formatting | bytes 131072
